TPU v7x, 1024 devices: a whole 4x8x16 slice. The times are simulated.
1024 devices in a mesh: lat: 32 (over y_hi, z), lon: 32 (over y_lo, x, core).
Axes of the slice: x: 4, y: 8 (y_hi: 2, y_lo: 4; y = y_hi * 4 + y_lo), z: 16, core: 2. Of those that a mesh axis runs over, the one named last changes fastest.
Arguments:
- query_field: bfloat16 [256, 512, 768], P('lat', 'lon'), may hold values from -6 to 6
- key_field: bfloat16 [256, 512, 768], P('lat', 'lon'), may hold values from -6 to 6
- value_field: bfloat16 [256, 512, 768], P('lat', 'lon'), may hold values from -12 to 12
- out_cotangent: bfloat16 [256, 512, 768], P('lat', 'lon'), may hold values from -16 to 16
Outputs:
- attended: bfloat16 [256, 512, 768], P('lat', 'lon')
- query_grad: bfloat16 [256, 512, 768], P('lat', 'lon')
- key_grad: bfloat16 [256, 512, 768], P('lat', 'lon')
- value_grad: bfloat16 [256, 512, 768], P('lat', 'lon')
All inputs are finite; a program needn't handle non-finite values.
Results may differ from a plain program's by a relative error of at most 0.025.
Values may be sent and summed in bfloat16 or wider, within the bound.
No kernel may reach another device: no remote copies, remote signals or barrier semaphores. Data moves between devices by JAX's collectives and lax.ppermute only.
A program may use at most 128 MiB of HBM per device.

v0:
```python
import jax
import jax.numpy as jnp
from jax import lax
from jax.experimental import pallas as pl
from jax.experimental.pallas import tpu as pltpu
from jax.sharding import PartitionSpec as P


HEAD_DIM = 64
TILE = 8
CELLS = TILE * TILE
BAND = 2 * CELLS
PAIR = 2 * HEAD_DIM
SCALE = HEAD_DIM**-0.5
FAR = -1e30
F32, BF16 = jnp.float32, jnp.bfloat16
UNROLL = 6


def dot(a, b):
    return jnp.dot(a, b, preferred_element_type=F32)


def tile_order(x, odd):
    west = x[:, :TILE].reshape(CELLS, x.shape[-1])
    east = x[:, TILE:].reshape(CELLS, x.shape[-1])
    return jnp.concatenate([jnp.where(odd, west, east), jnp.where(odd, east, west)], axis=0)


def grid_order(x, odd):
    first = x[:CELLS].reshape(TILE, TILE, x.shape[-1])
    second = x[CELLS:].reshape(TILE, TILE, x.shape[-1])
    return jnp.concatenate([jnp.where(odd, first, second), jnp.where(odd, second, first)], axis=1)


def below(shape, axis, bound):
    return lax.broadcasted_iota(jnp.int32, shape, axis) < bound


def wide(x):
    row = below(x.shape, 0, HEAD_DIM)
    return jnp.concatenate([jnp.where(row, x, 0.0), jnp.where(row, 0.0, x)], axis=1).astype(BF16)


def diagonal(x):
    return jnp.concatenate([x[:HEAD_DIM, :PAIR], x[HEAD_DIM:, PAIR : 2 * PAIR]], axis=0)


def by_head(x):
    return jnp.concatenate(
        [
            jnp.sum(x[:HEAD_DIM], axis=0, keepdims=True),
            jnp.sum(x[HEAD_DIM:], axis=0, keepdims=True),
        ],
        axis=1,
    )


def each_pair(width, step):
    def body(p, carry):
        step(p, pl.ds(pl.multiple_of(p * PAIR, PAIR), PAIR))
        return carry

    lax.fori_loop(0, width // PAIR, body, 0, unroll=UNROLL)


CORE, SIDE = 3 * BAND, 3 * CELLS


def beside_first(rows):
    return (lax.broadcasted_iota(jnp.int32, (rows, 2 * PAIR), 1) & CELLS) == 0


def near(x):
    sides = jnp.where(beside_first(SIDE), x[CORE : CORE + SIDE], x[CORE + SIDE :])
    return jnp.concatenate([x[:CORE], sides], axis=0)


def split(x):
    first, none = beside_first(x.shape[0]), jnp.zeros((), x.dtype)
    return [jnp.where(first, x, none), jnp.where(first, none, x)]


def attend_kernel(
    bias_ref, odd_ref, mine_ref, own_ref, even_ref, odds_ref, first_ref, second_ref, att_ref, stats_ref, low_ref
):
    odd = odd_ref[0] == 1
    refs = (own_ref, even_ref, odds_ref, first_ref, second_ref)

    def step(p, lanes):
        k_all = jnp.concatenate([ref[0, :, lanes] for ref in refs], axis=0)
        v_all = jnp.concatenate([ref[1, :, lanes] for ref in refs], axis=0)
        q_turn = mine_ref[0, :, lanes].astype(F32).T
        g_turn = mine_ref[1, :, lanes].astype(F32).T
        scores = near(dot(k_all, wide(q_turn)))
        cut, last = 2 * BAND, CORE + 2 * CELLS
        bias = bias_ref[0]
        scores = jnp.concatenate(
            [scores[:cut], scores[cut:CORE] + bias, scores[CORE:last], scores[last:] + bias], axis=0
        )
        peak = jnp.max(scores, axis=0, keepdims=True)
        raised = jnp.exp(scores - peak)
        total = jnp.sum(raised, axis=0, keepdims=True)
        low = (raised * (1.0 / total)).astype(BF16)
        low_ref[p] = low
        full = jnp.concatenate([low[:CORE], *split(low[CORE:])], axis=0)
        att_turn = diagonal(dot(v_all.T, full)).astype(BF16).astype(F32)
        att_ref[:, :, lanes] = grid_order(att_turn.T, odd).astype(BF16)
        drift = by_head(g_turn * att_turn)
        log_total = peak + jnp.log(total)
        stats_ref[p] = jnp.concatenate(
            [log_total[:, :PAIR], log_total[:, PAIR:], drift[:, :PAIR], drift[:, PAIR:], jnp.zeros((4, PAIR), F32)],
            axis=0,
        )

    each_pair(mine_ref.shape[-1], step)


def slope_kernel(
    odd_ref, mine_ref, own_ref, even_ref, odds_ref, first_ref, second_ref, stats_ref, low_ref, dq_ref, part_ref
):
    odd = odd_ref[0] == 1
    refs = (own_ref, even_ref, odds_ref, first_ref, second_ref)

    def step(p, lanes):
        k_all = jnp.concatenate([ref[0, :, lanes] for ref in refs], axis=0)
        v_all = jnp.concatenate([ref[1, :, lanes] for ref in refs], axis=0)
        q_mine, g_mine = mine_ref[0, :, lanes], mine_ref[1, :, lanes]
        stats = stats_ref[p]
        drift = jnp.concatenate([stats[2:3], stats[3:4]], axis=1)
        low = low_ref[p]
        slopes = (low.astype(F32) * (near(dot(v_all, wide(g_mine.astype(F32).T))) - drift)).astype(BF16)
        full = jnp.concatenate([slopes[:CORE], *split(slopes[CORE:])], axis=0)
        dq_turn = diagonal(dot(k_all.T, full)) * SCALE
        dq_ref[:, :, lanes] = grid_order(dq_turn.T, odd).astype(BF16)
        lane = below((PAIR, PAIR), 1, HEAD_DIM)
        for which, rows, mine in ((0, slopes, q_mine), (1, low, g_mine)):
            none = jnp.zeros((), BF16)
            tall = jnp.concatenate([jnp.where(lane, mine, none), jnp.where(lane, none, mine)], axis=0)
            rows = jnp.concatenate([rows[:BAND], *split(rows[CORE : CORE + CELLS])], axis=0)
            part_ref[which, :, lanes] = dot(rows, tall)

    each_pair(mine_ref.shape[-1], step)


def key_kernel(
    bias_ref, own_ref, first_ref, second_ref, even_ref, odds_ref, even_stats, odds_stats, part_ref,
    mid_ref, to_first_ref, to_second_ref,
):
    refs = (even_ref, odds_ref)

    def step(p, lanes):
        low_lane = below((PAIR, PAIR), 1, CELLS)
        low_row = below((PAIR, PAIR), 0, HEAD_DIM)

        def keys(which):
            own = own_ref[which, :, lanes].astype(F32).T
            both = jnp.concatenate(
                [first_ref[which, :CELLS, lanes], second_ref[which, :CELLS, lanes]], axis=0
            ).astype(F32).T
            turned = pltpu.roll(both, CELLS, axis=1)
            block = low_row == low_lane
            first = jnp.where(block, jnp.where(low_lane, both, turned), 0.0).astype(BF16)
            second = jnp.where(block, jnp.where(low_lane, turned, both), 0.0).astype(BF16)
            return jnp.concatenate([wide(own), first, second], axis=1)

        def beside(x):
            sides = [
                x[at * CELLS : (at + 1) * CELLS, (2 + at % 2) * PAIR : (3 + at % 2) * PAIR] for at in range(4)
            ]
            return jnp.concatenate([x[:, : 2 * PAIR], jnp.concatenate(sides, axis=0)], axis=1)

        def spread(x):
            x = x.astype(BF16)
            none = jnp.zeros((CELLS, PAIR), BF16)
            sides = [x[at * CELLS : (at + 1) * CELLS, 2 * PAIR :] for at in range(4)]
            first = jnp.concatenate([none if at % 2 else sides[at] for at in range(4)], axis=0)
            second = jnp.concatenate([sides[at] if at % 2 else none for at in range(4)], axis=0)
            return jnp.concatenate([x[:, : 2 * PAIR], first, second], axis=1)

        stats = [ref[p] for ref in (even_stats, odds_stats)]
        columns = jnp.concatenate(stats + [jnp.zeros((PAIR - 16, PAIR), F32)], axis=0).T

        def column(base):
            rows = []
            for at in range(2):
                head0 = jnp.broadcast_to(columns[:, 8 * at + base : 8 * at + base + 1], (PAIR, PAIR))
                head1 = jnp.broadcast_to(columns[:, 8 * at + base + 1 : 8 * at + base + 2], (PAIR, PAIR))
                rows.append(jnp.concatenate([head0, head1, jnp.where(low_lane, head0, head1)], axis=1))
            return jnp.concatenate(rows, axis=0)

        def store(which, x):
            part = part_ref[which, :, lanes]
            mid_ref[which, :, lanes] = part[:BAND] + diagonal(x).T
            first, second = x[:, 2 * PAIR : 3 * PAIR], x[:, 3 * PAIR :]
            first = jnp.where(low_row, first, pltpu.roll(first, CELLS, axis=1))
            second = jnp.where(low_row, pltpu.roll(second, CELLS, axis=1), second)
            both = (part[BAND:] + jnp.where(low_lane, first, second).T).astype(BF16)
            to_first_ref[which, :, lanes] = both[:CELLS]
            to_second_ref[which, :, lanes] = both[CELLS:]

        q_all = jnp.concatenate([ref[0, :, lanes] for ref in refs], axis=0)
        g_all = jnp.concatenate([ref[1, :, lanes] for ref in refs], axis=0)
        scores = beside(dot(q_all, keys(0)))
        scores = jnp.concatenate([scores[:BAND], scores[BAND:] + bias_ref[0]], axis=0)
        weights = jnp.exp(scores - column(0))
        store(1, dot(g_all.T, spread(weights)))
        slopes = weights * (beside(dot(g_all, keys(1))) - column(2))
        store(0, dot(q_all.T, spread(slopes)))

    each_pair(own_ref.shape[-1], step)


def order_kernel(odd_ref, q_ref, g_ref, out_ref):
    odd = odd_ref[0] == 1
    out_ref[0] = (tile_order(q_ref[...].astype(F32), odd) * SCALE).astype(BF16)
    out_ref[1] = tile_order(g_ref[...].astype(F32), odd).astype(BF16)


def pack_kernel(odd_ref, own_ref, even_ref, odds_ref, first_ref, second_ref):
    odd = odd_ref[0] == 1
    for which in range(2):
        for band, ref in enumerate((own_ref, even_ref, odds_ref)):
            x = ref[which].astype(F32).reshape(TILE, 2 * TILE, ref.shape[-1])
            ordered = tile_order(x, odd).astype(BF16)
            first_ref[which, band * CELLS : (band + 1) * CELLS] = ordered[:CELLS]
            second_ref[which, band * CELLS : (band + 1) * CELLS] = ordered[CELLS:]


def finish_kernel(odd_ref, mid_ref, first_ref, second_ref, dk_ref, dv_ref):
    odd = odd_ref[0] == 1
    for which, out in ((0, dk_ref), (1, dv_ref)):
        sides = jnp.concatenate([first_ref[which], second_ref[which]], axis=0).astype(F32)
        mid = mid_ref[which].reshape(TILE, 2 * TILE, mid_ref.shape[-1])
        out[...] = (mid + grid_order(sides, odd)).astype(BF16)


def call(kernel, scalars, arrays, outs, flops, moved):
    return pl.pallas_call(
        kernel,
        in_specs=[pl.BlockSpec(memory_space=pltpu.SMEM)] * len(scalars)
        + [pl.BlockSpec(memory_space=pltpu.VMEM)] * len(arrays),
        out_specs=[pl.BlockSpec(memory_space=pltpu.VMEM)] * len(outs),
        out_shape=[jax.ShapeDtypeStruct(*out) for out in outs],
        compiler_params=pltpu.CompilerParams(vmem_limit_bytes=32 << 20),
        cost_estimate=pl.CostEstimate(flops=flops, bytes_accessed=moved, transcendentals=0),
    )(*scalars, *arrays)


def swap(value, axis, start, closed):
    count = lax.axis_size(axis)
    pairs = []
    for low in range(start, count if closed else count - 1, 2):
        high = (low + 1) % count
        pairs += [(low, high), (high, low)]
    return lax.ppermute(value, axis, pairs)


def block(query_field, key_field, value_field, out_cotangent):
    band = lax.axis_index("lat")
    edge = (band == 0) | (band == lax.axis_size("lat") - 1)
    bias = jnp.where(edge, FAR, 0.0).astype(F32)[None]
    odd = (lax.axis_index("lon") % 2).astype(jnp.int32)[None]
    field, width = query_field.shape, query_field.shape[-1]
    pairs = width // PAIR
    keys = jnp.stack([key_field.reshape(BAND, width), value_field.reshape(BAND, width)])
    keys_even = swap(keys, "lat", 0, False)
    keys_odd = swap(keys, "lat", 1, False)
    (queries,) = call(order_kernel, [odd], [query_field, out_cotangent], [((2, BAND, width), BF16)], 1 << 20, 1 << 20)
    queries_even = swap(queries, "lat", 0, False)
    queries_odd = swap(queries, "lat", 1, False)
    column = ((2, 3 * CELLS, width), BF16)
    first, second = call(pack_kernel, [odd], [keys, keys_even, keys_odd], [column, column], 1 << 20, 2 << 20)
    keys_second = swap(second, "lon", 1, True)
    keys_first = swap(first, "lon", 0, True)
    around = [queries, keys, keys_even, keys_odd, keys_first, keys_second]
    att, stats, low = call(
        attend_kernel, [bias, odd], around,
        [(field, BF16), ((pairs, 8, PAIR), F32), ((pairs, CORE + SIDE, 2 * PAIR), BF16)], 1 << 30, 8 << 20,
    )
    stats_odd = swap(stats, "lat", 1, False)
    stats_even = swap(stats, "lat", 0, False)
    dq, part = call(
        slope_kernel, [odd], [*around, stats, low],
        [(field, BF16), ((2, 2 * BAND, width), F32)], 1 << 30, 8 << 20,
    )
    tile = ((2, CELLS, width), BF16)
    mid, first, second = call(
        key_kernel, [bias],
        [keys, keys_first, keys_second, queries_even, queries_odd, stats_even, stats_odd, part],
        [((2, BAND, width), F32), tile, tile], 1 << 30, 8 << 20,
    )
    from_second = swap(second, "lon", 1, True)
    from_first = swap(first, "lon", 0, True)
    dk, dv = call(
        finish_kernel, [odd], [mid, from_first, from_second], [(field, BF16), (field, BF16)], 1 << 20, 2 << 20
    )
    return att, dq, dk, dv


def solution(mesh):
    spec = P("lat", "lon", None)
    return jax.shard_map(block, mesh=mesh, in_specs=(spec,) * 4, out_specs=(spec,) * 4, check_vma=False)
```

profile of v0, /device:TPU:55, one launch (start us, length us, event | category | flops | bytes accessed | tf_op | source)
XLA Modules:
  0.0 97.1 jit_solution(3250691779829334920)
XLA Ops:
  0.6 0.0 copy-start
  0.6 0.0 copy-start.1
  0.7 1.1 %pad_maximum_fusion.own_ref = bf16[2,128,768]{2,1,0:T(8,128)(2,1)S(1)} fusion(bf16[1,128,768]{2,1,0:T(8,128)(2,1)} %bitcast.4, bf16[1,128,768]{2,1,0:T(8,128)(2,1)} %bitcast.5), kind=kLoop, calls=%fused_computation | loop fusion | flops 196608 | bytes 786432 | tf_op jit(solution)/shard_map/stack | solution.py:266
  1.8 4.0 %collective-permute-start = (bf16[2,128,768]{2,1,0:T(8,128)(2,1)S(1)}, bf16[2,128,768]{2,1,0:T(8,128)(2,1)S(1)}, u32[]{:S(2)}, u32[]{:S(2)}) collective-permute-start(bf16[2,128,768]{2,1,0:T(8,128)(2,1)S(1)} %pad_maximum_fusion.own_ref), channel_id=1, source_target_pairs={{0,32},{32,0},{64,96},{96,64},{128,160},{160,128},{192,224},{224,1... | collective-permute-start | bytes 1179656 | tf_op jit(solution)/shard_map/ppermute | solution.py:256
  5.8 17.5 %collective-permute-start.1 = (bf16[2,128,768]{2,1,0:T(8,128)(2,1)S(1)}, bf16[2,128,768]{2,1,0:T(8,128)(2,1)S(1)}, u32[]{:S(2)}, u32[]{:S(2)}) collective-permute-start(bf16[2,128,768]{2,1,0:T(8,128)(2,1)S(1)} %pad_maximum_fusion.own_ref), channel_id=1, source_target_pairs={{32,64},{64,32},{96,128},{128,96},{160,192},{192,160},{224,256},{2... | collective-permute-start | bytes 1179656 | tf_op jit(solution)/shard_map/ppermute | solution.py:256
  23.3 0.0 collective-permute-done.even_ref
  23.3 15.8 %collective-permute-done.1.odds_ref = bf16[2,128,768]{2,1,0:T(8,128)(2,1)S(1)} collective-permute-done((bf16[2,128,768]{2,1,0:T(8,128)(2,1)S(1)}, bf16[2,128,768]{2,1,0:T(8,128)(2,1)S(1)}, u32[]{:S(2)}, u32[]{:S(2)}) %collective-permute-start.1) | collective-permute-done | bytes 393248 | tf_op jit(solution)/shard_map/ppermute | solution.py:256
  39.1 1.3 %shard_map.76 = (bf16[2,192,768]{2,1,0:T(8,128)(2,1)}, bf16[2,192,768]{2,1,0:T(8,128)(2,1)}) custom-call(s32[1]{0:T(128)} %bitcast.1.odd_ref, bf16[2,128,768]{2,1,0:T(8,128)(2,1)S(1)} %pad_maximum_fusion.own_ref, bf16[2,128,768]{2,1,0:T(8,128)(2,1)S(1)} %collective-permute-done.even_ref, bf16[2,128,768]{2,1,0:T(8,128)(2,1)S(1)} %collective-permute-done.1.odds_ref), custom_call_target="tpu_custom_call" | custom-call | flops 1048576 | bytes 2097152 | tf_op jit(solution)/shard_map/pallas_call | solution.py:239
  40.3 4.4 %collective-permute-start.2 = (bf16[2,192,768]{2,1,0:T(8,128)(2,1)}, bf16[2,192,768]{2,1,0:T(8,128)(2,1)S(1)}, u32[]{:S(2)}, u32[]{:S(2)}) collective-permute-start(bf16[2,192,768]{2,1,0:T(8,128)(2,1)} %get-tuple-element.16), channel_id=1, source_target_pairs={{0,1},{1,0},{2,3},{3,2},{4,5},{5,4},{6,7},{7,6},{8,9},{9,8},{10,11... | collective-permute-start | bytes 1769480 | tf_op jit(solution)/shard_map/ppermute | solution.py:256
  44.8 1.9 %collective-permute-start.3 = (bf16[2,192,768]{2,1,0:T(8,128)(2,1)}, bf16[2,192,768]{2,1,0:T(8,128)(2,1)S(1)}, u32[]{:S(2)}, u32[]{:S(2)}) collective-permute-start(bf16[2,192,768]{2,1,0:T(8,128)(2,1)} %get-tuple-element.17), channel_id=1, source_target_pairs={{1,2},{2,1},{3,4},{4,3},{5,6},{6,5},{7,8},{8,7},{9,10},{10,9},{11,... | collective-permute-start | bytes 1769480 | tf_op jit(solution)/shard_map/ppermute | solution.py:256
  46.7 0.0 copy-done
  46.7 0.0 copy-done.1
  46.7 0.1 shard_map.75.mine_ref
  46.8 1.9 %collective-permute-start.4 = (bf16[2,128,768]{2,1,0:T(8,128)(2,1)S(1)}, bf16[2,128,768]{2,1,0:T(8,128)(2,1)S(1)}, u32[]{:S(2)}, u32[]{:S(2)}) collective-permute-start(bf16[2,128,768]{2,1,0:T(8,128)(2,1)S(1)} %shard_map.75.mine_ref), channel_id=1, source_target_pairs={{0,32},{32,0},{64,96},{96,64},{128,160},{160,128},{192,224},{224,1... | collective-permute-start | bytes 1179656 | tf_op jit(solution)/shard_map/ppermute | solution.py:256
  48.8 9.4 %collective-permute-start.5 = (bf16[2,128,768]{2,1,0:T(8,128)(2,1)S(1)}, bf16[2,128,768]{2,1,0:T(8,128)(2,1)S(1)}, u32[]{:S(2)}, u32[]{:S(2)}) collective-permute-start(bf16[2,128,768]{2,1,0:T(8,128)(2,1)S(1)} %shard_map.75.mine_ref), channel_id=1, source_target_pairs={{32,64},{64,32},{96,128},{128,96},{160,192},{192,160},{224,256},{2... | collective-permute-start | bytes 1179656 | tf_op jit(solution)/shard_map/ppermute | solution.py:256
  58.2 0.0 collective-permute-done.2.first_ref
  58.2 3.3 %collective-permute-done.3.second_ref = bf16[2,192,768]{2,1,0:T(8,128)(2,1)S(1)} collective-permute-done((bf16[2,192,768]{2,1,0:T(8,128)(2,1)}, bf16[2,192,768]{2,1,0:T(8,128)(2,1)S(1)}, u32[]{:S(2)}, u32[]{:S(2)}) %collective-permute-start.3) | collective-permute-done | bytes 589856 | tf_op jit(solution)/shard_map/ppermute | solution.py:256
  61.5 4.6 %shard_map.77 = (bf16[8,16,768]{2,1,0:T(8,128)(2,1)}, f32[6,8,128]{2,1,0:T(8,128)S(1)}, bf16[6,576,256]{2,1,0:T(8,128)(2,1)S(1)}) custom-call(f32[1]{0:T(128)} %bitcast.bias_ref, s32[1]{0:T(128)} %bitcast.1.odd_ref, bf16[2,128,768]{2,1,0:T(8,128)(2,1)S(1)} %shard_map.75.mine_ref, bf16[2,128,768]{2,1,0:T(8,128)(2,1)S(1)} %pad_maximum_fusion.own_ref, ...), custom_call_target="tpu_custom_call" | custom-call | flops 1073741824 | bytes 8388608 | tf_op jit(solution)/shard_map/pallas_call | solution.py:239
  66.1 1.9 %collective-permute-start.6 = (f32[6,8,128]{2,1,0:T(8,128)S(1)}, f32[6,8,128]{2,1,0:T(8,128)S(1)}, u32[]{:S(2)}, u32[]{:S(2)}) collective-permute-start(f32[6,8,128]{2,1,0:T(8,128)S(1)} %get-tuple-element.19.stats_ref), channel_id=1, source_target_pairs={{0,32},{32,0},{64,96},{96,64},{128,160},{160,128},{192,224},{224,1... | collective-permute-start | bytes 73736 | tf_op jit(solution)/shard_map/ppermute | solution.py:256
  68.0 9.4 %collective-permute-start.7 = (f32[6,8,128]{2,1,0:T(8,128)S(1)}, f32[6,8,128]{2,1,0:T(8,128)S(1)}, u32[]{:S(2)}, u32[]{:S(2)}) collective-permute-start(f32[6,8,128]{2,1,0:T(8,128)S(1)} %get-tuple-element.19.stats_ref), channel_id=1, source_target_pairs={{32,64},{64,32},{96,128},{128,96},{160,192},{192,160},{224,256},{2... | collective-permute-start | bytes 73736 | tf_op jit(solution)/shard_map/ppermute | solution.py:256
  77.4 3.4 %shard_map.78 = (bf16[8,16,768]{2,1,0:T(8,128)(2,1)}, f32[2,256,768]{2,1,0:T(8,128)S(1)}) custom-call(s32[1]{0:T(128)} %bitcast.1.odd_ref, bf16[2,128,768]{2,1,0:T(8,128)(2,1)S(1)} %shard_map.75.mine_ref, bf16[2,128,768]{2,1,0:T(8,128)(2,1)S(1)} %pad_maximum_fusion.own_ref, bf16[2,128,768]{2,1,0:T(8,128)(2,1)S(1)} %collective-permute-done.even_ref, ...), custom_call_target="tpu_custom_call" | custom-call | flops 1073741824 | bytes 8388608 | tf_op jit(solution)/shard_map/pallas_call | solution.py:239
  80.8 0.0 collective-permute-done.4.even_ref
  80.8 0.0 collective-permute-done.5.odds_ref
  80.8 0.0 collective-permute-done.6.even_stats
  80.8 0.0 collective-permute-done.7.odds_stats
  80.8 4.4 %shard_map.79 = (f32[2,128,768]{2,1,0:T(8,128)S(1)}, bf16[2,64,768]{2,1,0:T(8,128)(2,1)S(1)}, bf16[2,64,768]{2,1,0:T(8,128)(2,1)S(1)}) custom-call(f32[1]{0:T(128)} %bitcast.bias_ref, bf16[2,128,768]{2,1,0:T(8,128)(2,1)S(1)} %pad_maximum_fusion.own_ref, bf16[2,192,768]{2,1,0:T(8,128)(2,1)S(1)} %collective-permute-done.2.first_ref, ...), custom_call_target="tpu_custom_call" | custom-call | flops 1073741824 | bytes 8388608 | tf_op jit(solution)/shard_map/pallas_call | solution.py:239
  85.3 1.9 %collective-permute-start.8 = (bf16[2,64,768]{2,1,0:T(8,128)(2,1)S(1)}, bf16[2,64,768]{2,1,0:T(8,128)(2,1)S(1)}, u32[]{:S(2)}, u32[]{:S(2)}) collective-permute-start(bf16[2,64,768]{2,1,0:T(8,128)(2,1)S(1)} %get-tuple-element.24), channel_id=1, source_target_pairs={{0,1},{1,0},{2,3},{3,2},{4,5},{5,4},{6,7},{7,6},{8,9},{9,8},{10,11... | collective-permute-start | bytes 589832 | tf_op jit(solution)/shard_map/ppermute | solution.py:256
  87.2 1.9 %collective-permute-start.9 = (bf16[2,64,768]{2,1,0:T(8,128)(2,1)S(1)}, bf16[2,64,768]{2,1,0:T(8,128)(2,1)S(1)}, u32[]{:S(2)}, u32[]{:S(2)}) collective-permute-start(bf16[2,64,768]{2,1,0:T(8,128)(2,1)S(1)} %get-tuple-element.25), channel_id=1, source_target_pairs={{1,2},{2,1},{3,4},{4,3},{5,6},{6,5},{7,8},{8,7},{9,10},{10,9},{11,... | collective-permute-start | bytes 589832 | tf_op jit(solution)/shard_map/ppermute | solution.py:256
  89.1 0.0 collective-permute-done.8.first_ref
  89.1 7.2 %collective-permute-done.9.second_ref = bf16[2,64,768]{2,1,0:T(8,128)(2,1)S(1)} collective-permute-done((bf16[2,64,768]{2,1,0:T(8,128)(2,1)S(1)}, bf16[2,64,768]{2,1,0:T(8,128)(2,1)S(1)}, u32[]{:S(2)}, u32[]{:S(2)}) %collective-permute-start.9) | collective-permute-done | bytes 196640 | tf_op jit(solution)/shard_map/ppermute | solution.py:256
  96.3 0.8 shard_map.80
Async XLA Ops:
  0.6 46.1 %copy-start = (bf16[8,16,768]{2,1,0:T(8,128)(2,1)S(1)}, bf16[8,16,768]{2,1,0:T(8,128)(2,1)}, u32[]{:S(2)}) copy-start(bf16[8,16,768]{2,1,0:T(8,128)(2,1)} %q_ref.1) | copy-start | bytes 589828
  0.6 46.1 %copy-start.1 = (bf16[8,16,768]{2,1,0:T(8,128)(2,1)S(1)}, bf16[8,16,768]{2,1,0:T(8,128)(2,1)}, u32[]{:S(2)}) copy-start(bf16[8,16,768]{2,1,0:T(8,128)(2,1)} %g_ref.1) | copy-start | bytes 589828
  1.8 21.5 %collective-permute-start = (bf16[2,128,768]{2,1,0:T(8,128)(2,1)S(1)}, bf16[2,128,768]{2,1,0:T(8,128)(2,1)S(1)}, u32[]{:S(2)}, u32[]{:S(2)}) collective-permute-start(bf16[2,128,768]{2,1,0:T(8,128)(2,1)S(1)} %pad_maximum_fusion.own_ref), channel_id=1, source_target_pairs={{0,32},{32,0},{64,96},{96,64},{128,160},{160,128},{192,224},{224,1... | collective-permute-start | bytes 1179656 | tf_op jit(solution)/shard_map/ppermute | solution.py:256
  5.8 33.3 %collective-permute-start.1 = (bf16[2,128,768]{2,1,0:T(8,128)(2,1)S(1)}, bf16[2,128,768]{2,1,0:T(8,128)(2,1)S(1)}, u32[]{:S(2)}, u32[]{:S(2)}) collective-permute-start(bf16[2,128,768]{2,1,0:T(8,128)(2,1)S(1)} %pad_maximum_fusion.own_ref), channel_id=1, source_target_pairs={{32,64},{64,32},{96,128},{128,96},{160,192},{192,160},{224,256},{2... | collective-permute-start | bytes 1179656 | tf_op jit(solution)/shard_map/ppermute | solution.py:256
  40.3 17.8 %collective-permute-start.2 = (bf16[2,192,768]{2,1,0:T(8,128)(2,1)}, bf16[2,192,768]{2,1,0:T(8,128)(2,1)S(1)}, u32[]{:S(2)}, u32[]{:S(2)}) collective-permute-start(bf16[2,192,768]{2,1,0:T(8,128)(2,1)} %get-tuple-element.16), channel_id=1, source_target_pairs={{0,1},{1,0},{2,3},{3,2},{4,5},{5,4},{6,7},{7,6},{8,9},{9,8},{10,11... | collective-permute-start | bytes 1769480 | tf_op jit(solution)/shard_map/ppermute | solution.py:256
  44.8 16.7 %collective-permute-start.3 = (bf16[2,192,768]{2,1,0:T(8,128)(2,1)}, bf16[2,192,768]{2,1,0:T(8,128)(2,1)S(1)}, u32[]{:S(2)}, u32[]{:S(2)}) collective-permute-start(bf16[2,192,768]{2,1,0:T(8,128)(2,1)} %get-tuple-element.17), channel_id=1, source_target_pairs={{1,2},{2,1},{3,4},{4,3},{5,6},{6,5},{7,8},{8,7},{9,10},{10,9},{11,... | collective-permute-start | bytes 1769480 | tf_op jit(solution)/shard_map/ppermute | solution.py:256
  46.8 34.0 %collective-permute-start.4 = (bf16[2,128,768]{2,1,0:T(8,128)(2,1)S(1)}, bf16[2,128,768]{2,1,0:T(8,128)(2,1)S(1)}, u32[]{:S(2)}, u32[]{:S(2)}) collective-permute-start(bf16[2,128,768]{2,1,0:T(8,128)(2,1)S(1)} %shard_map.75.mine_ref), channel_id=1, source_target_pairs={{0,32},{32,0},{64,96},{96,64},{128,160},{160,128},{192,224},{224,1... | collective-permute-start | bytes 1179656 | tf_op jit(solution)/shard_map/ppermute | solution.py:256
  48.8 32.0 %collective-permute-start.5 = (bf16[2,128,768]{2,1,0:T(8,128)(2,1)S(1)}, bf16[2,128,768]{2,1,0:T(8,128)(2,1)S(1)}, u32[]{:S(2)}, u32[]{:S(2)}) collective-permute-start(bf16[2,128,768]{2,1,0:T(8,128)(2,1)S(1)} %shard_map.75.mine_ref), channel_id=1, source_target_pairs={{32,64},{64,32},{96,128},{128,96},{160,192},{192,160},{224,256},{2... | collective-permute-start | bytes 1179656 | tf_op jit(solution)/shard_map/ppermute | solution.py:256
  66.1 14.7 %collective-permute-start.6 = (f32[6,8,128]{2,1,0:T(8,128)S(1)}, f32[6,8,128]{2,1,0:T(8,128)S(1)}, u32[]{:S(2)}, u32[]{:S(2)}) collective-permute-start(f32[6,8,128]{2,1,0:T(8,128)S(1)} %get-tuple-element.19.stats_ref), channel_id=1, source_target_pairs={{0,32},{32,0},{64,96},{96,64},{128,160},{160,128},{192,224},{224,1... | collective-permute-start | bytes 73736 | tf_op jit(solution)/shard_map/ppermute | solution.py:256
  68.0 12.8 %collective-permute-start.7 = (f32[6,8,128]{2,1,0:T(8,128)S(1)}, f32[6,8,128]{2,1,0:T(8,128)S(1)}, u32[]{:S(2)}, u32[]{:S(2)}) collective-permute-start(f32[6,8,128]{2,1,0:T(8,128)S(1)} %get-tuple-element.19.stats_ref), channel_id=1, source_target_pairs={{32,64},{64,32},{96,128},{128,96},{160,192},{192,160},{224,256},{2... | collective-permute-start | bytes 73736 | tf_op jit(solution)/shard_map/ppermute | solution.py:256
  85.3 3.9 %collective-permute-start.8 = (bf16[2,64,768]{2,1,0:T(8,128)(2,1)S(1)}, bf16[2,64,768]{2,1,0:T(8,128)(2,1)S(1)}, u32[]{:S(2)}, u32[]{:S(2)}) collective-permute-start(bf16[2,64,768]{2,1,0:T(8,128)(2,1)S(1)} %get-tuple-element.24), channel_id=1, source_target_pairs={{0,1},{1,0},{2,3},{3,2},{4,5},{5,4},{6,7},{7,6},{8,9},{9,8},{10,11... | collective-permute-start | bytes 589832 | tf_op jit(solution)/shard_map/ppermute | solution.py:256
  87.2 9.1 %collective-permute-start.9 = (bf16[2,64,768]{2,1,0:T(8,128)(2,1)S(1)}, bf16[2,64,768]{2,1,0:T(8,128)(2,1)S(1)}, u32[]{:S(2)}, u32[]{:S(2)}) collective-permute-start(bf16[2,64,768]{2,1,0:T(8,128)(2,1)S(1)} %get-tuple-element.25), channel_id=1, source_target_pairs={{1,2},{2,1},{3,4},{4,3},{5,6},{6,5},{7,8},{8,7},{9,10},{10,9},{11,... | collective-permute-start | bytes 589832 | tf_op jit(solution)/shard_map/ppermute | solution.py:256
where the time goes:
time: 97.5 us; the launch traced here: 97.1 us
  starting transfers between devices  54.2 us (56%)
  waiting for transfers between devices  26.3 us (27%)
  Pallas kernels  14.6 us (15%)
  other arithmetic  1.11 us (1%)
    ppermute x10, starting transfers between devices, swap(): return lax.ppermute(value, axis, pairs)  54.2 us
    ppermute x10, waiting for transfers between devices, swap(): return lax.ppermute(value, axis, pairs)  26.3 us
    pallas_call x6, Pallas kernels, call(): pl.pallas_call(kernel, in_specs=[pl.BlockSpec(memory_space=pltpu.SMEM)] *...  14.6 us
  transfers between devices with their start and end apart: 10, of which 3 were waited for; matrix products, arithmetic and copies ran while one was open for 0% of the time, Pallas kernels for 8%

commit v1 on v0

--- a/solution.py
+++ b/solution.py
@@ -82,10 +82,11 @@
 
 
 def attend_kernel(
-    bias_ref, odd_ref, mine_ref, own_ref, even_ref, odds_ref, first_ref, second_ref, att_ref, stats_ref, low_ref
+    bias_ref, odd_ref, mine_ref, own_ref, even_ref, odds_ref,
+    first_ref, first_odds_ref, second_ref, second_odds_ref, att_ref, stats_ref, low_ref,
 ):
     odd = odd_ref[0] == 1
-    refs = (own_ref, even_ref, odds_ref, first_ref, second_ref)
+    refs = (own_ref, even_ref, odds_ref, first_ref, first_odds_ref, second_ref, second_odds_ref)
 
     def step(p, lanes):
         k_all = jnp.concatenate([ref[0, :, lanes] for ref in refs], axis=0)
@@ -117,10 +118,11 @@
 
 
 def slope_kernel(
-    odd_ref, mine_ref, own_ref, even_ref, odds_ref, first_ref, second_ref, stats_ref, low_ref, dq_ref, part_ref
+    odd_ref, mine_ref, own_ref, even_ref, odds_ref,
+    first_ref, first_odds_ref, second_ref, second_odds_ref, stats_ref, low_ref, dq_ref, part_ref,
 ):
     odd = odd_ref[0] == 1
-    refs = (own_ref, even_ref, odds_ref, first_ref, second_ref)
+    refs = (own_ref, even_ref, odds_ref, first_ref, first_odds_ref, second_ref, second_odds_ref)
 
     def step(p, lanes):
         k_all = jnp.concatenate([ref[0, :, lanes] for ref in refs], axis=0)
@@ -137,77 +139,103 @@
         for which, rows, mine in ((0, slopes, q_mine), (1, low, g_mine)):
             none = jnp.zeros((), BF16)
             tall = jnp.concatenate([jnp.where(lane, mine, none), jnp.where(lane, none, mine)], axis=0)
-            rows = jnp.concatenate([rows[:BAND], *split(rows[CORE : CORE + CELLS])], axis=0)
-            part_ref[which, :, lanes] = dot(rows, tall)
+            part_ref[which, :, lanes] = dot(rows[:BAND], tall)
 
     each_pair(mine_ref.shape[-1], step)
 
 
-def key_kernel(
-    bias_ref, own_ref, first_ref, second_ref, even_ref, odds_ref, even_stats, odds_stats, part_ref,
-    mid_ref, to_first_ref, to_second_ref,
+def stat_columns(refs, p):
+    stats = [ref[p] for ref in refs]
+    turned = jnp.concatenate(stats + [jnp.zeros((PAIR - 8 * len(refs), PAIR), F32)], axis=0).T
+
+    def column(at, row):
+        return jnp.broadcast_to(turned[:, 8 * at + row : 8 * at + row + 1], (PAIR, PAIR))
+
+    return column
+
+
+def side_kernel(
+    bias_ref, first_ref, second_ref, mine_ref, even_ref, odds_ref, mine_stats, even_stats, odds_stats,
+    to_first_ref, to_second_ref,
 ):
-    refs = (even_ref, odds_ref)
+    refs = (mine_ref, even_ref, odds_ref)
+    blocks = range(2 * len(refs))
 
     def step(p, lanes):
         low_lane = below((PAIR, PAIR), 1, CELLS)
         low_row = below((PAIR, PAIR), 0, HEAD_DIM)
 
         def keys(which):
-            own = own_ref[which, :, lanes].astype(F32).T
             both = jnp.concatenate(
                 [first_ref[which, :CELLS, lanes], second_ref[which, :CELLS, lanes]], axis=0
             ).astype(F32).T
             turned = pltpu.roll(both, CELLS, axis=1)
             block = low_row == low_lane
-            first = jnp.where(block, jnp.where(low_lane, both, turned), 0.0).astype(BF16)
-            second = jnp.where(block, jnp.where(low_lane, turned, both), 0.0).astype(BF16)
-            return jnp.concatenate([wide(own), first, second], axis=1)
+            first = jnp.where(block, jnp.where(low_lane, both, turned), 0.0)
+            second = jnp.where(block, jnp.where(low_lane, turned, both), 0.0)
+            return jnp.concatenate([first, second], axis=1).astype(BF16)
 
         def beside(x):
-            sides = [
-                x[at * CELLS : (at + 1) * CELLS, (2 + at % 2) * PAIR : (3 + at % 2) * PAIR] for at in range(4)
-            ]
-            return jnp.concatenate([x[:, : 2 * PAIR], jnp.concatenate(sides, axis=0)], axis=1)
+            return jnp.concatenate(
+                [x[at * CELLS : (at + 1) * CELLS, at % 2 * PAIR : (1 + at % 2) * PAIR] for at in blocks], axis=0
+            )
 
         def spread(x):
             x = x.astype(BF16)
             none = jnp.zeros((CELLS, PAIR), BF16)
-            sides = [x[at * CELLS : (at + 1) * CELLS, 2 * PAIR :] for at in range(4)]
-            first = jnp.concatenate([none if at % 2 else sides[at] for at in range(4)], axis=0)
-            second = jnp.concatenate([sides[at] if at % 2 else none for at in range(4)], axis=0)
-            return jnp.concatenate([x[:, : 2 * PAIR], first, second], axis=1)
-
-        stats = [ref[p] for ref in (even_stats, odds_stats)]
-        columns = jnp.concatenate(stats + [jnp.zeros((PAIR - 16, PAIR), F32)], axis=0).T
-
-        def column(base):
-            rows = []
-            for at in range(2):
-                head0 = jnp.broadcast_to(columns[:, 8 * at + base : 8 * at + base + 1], (PAIR, PAIR))
-                head1 = jnp.broadcast_to(columns[:, 8 * at + base + 1 : 8 * at + base + 2], (PAIR, PAIR))
-                rows.append(jnp.concatenate([head0, head1, jnp.where(low_lane, head0, head1)], axis=1))
-            return jnp.concatenate(rows, axis=0)
+            rows = [x[at * CELLS : (at + 1) * CELLS] for at in blocks]
+            first = jnp.concatenate([none if at % 2 else rows[at] for at in blocks], axis=0)
+            second = jnp.concatenate([rows[at] if at % 2 else none for at in blocks], axis=0)
+            return jnp.concatenate([first, second], axis=1)
 
         def store(which, x):
-            part = part_ref[which, :, lanes]
-            mid_ref[which, :, lanes] = part[:BAND] + diagonal(x).T
-            first, second = x[:, 2 * PAIR : 3 * PAIR], x[:, 3 * PAIR :]
+            first, second = x[:, :PAIR], x[:, PAIR:]
             first = jnp.where(low_row, first, pltpu.roll(first, CELLS, axis=1))
             second = jnp.where(low_row, pltpu.roll(second, CELLS, axis=1), second)
-            both = (part[BAND:] + jnp.where(low_lane, first, second).T).astype(BF16)
+            both = jnp.where(low_lane, first, second).T.astype(BF16)
             to_first_ref[which, :, lanes] = both[:CELLS]
             to_second_ref[which, :, lanes] = both[CELLS:]
+
+        stat = stat_columns((mine_stats, even_stats, odds_stats), p)
+
+        def column(base):
+            return jnp.concatenate(
+                [jnp.where(low_lane, stat(at, base), stat(at, base + 1)) for at in range(len(refs))], axis=0
+            )
 
         q_all = jnp.concatenate([ref[0, :, lanes] for ref in refs], axis=0)
         g_all = jnp.concatenate([ref[1, :, lanes] for ref in refs], axis=0)
         scores = beside(dot(q_all, keys(0)))
-        scores = jnp.concatenate([scores[:BAND], scores[BAND:] + bias_ref[0]], axis=0)
+        scores = jnp.concatenate([scores[: 2 * BAND], scores[2 * BAND :] + bias_ref[0]], axis=0)
         weights = jnp.exp(scores - column(0))
         store(1, dot(g_all.T, spread(weights)))
         slopes = weights * (beside(dot(g_all, keys(1))) - column(2))
         store(0, dot(q_all.T, spread(slopes)))
 
+    each_pair(mine_ref.shape[-1], step)
+
+
+def own_kernel(bias_ref, own_ref, even_ref, odds_ref, even_stats, odds_stats, part_ref, mid_ref):
+    refs = (even_ref, odds_ref)
+
+    def step(p, lanes):
+        stat = stat_columns((even_stats, odds_stats), p)
+
+        def column(base):
+            return jnp.concatenate(
+                [jnp.concatenate([stat(at, base), stat(at, base + 1)], axis=1) for at in range(len(refs))], axis=0
+            )
+
+        q_all = jnp.concatenate([ref[0, :, lanes] for ref in refs], axis=0)
+        g_all = jnp.concatenate([ref[1, :, lanes] for ref in refs], axis=0)
+        scores = dot(q_all, wide(own_ref[0, :, lanes].astype(F32).T))
+        scores = jnp.concatenate([scores[:BAND], scores[BAND:] + bias_ref[0]], axis=0)
+        weights = jnp.exp(scores - column(0))
+        mid_ref[1, :, lanes] = part_ref[1, :, lanes] + diagonal(dot(g_all.T, weights.astype(BF16))).T
+        products = dot(g_all, wide(own_ref[1, :, lanes].astype(F32).T))
+        slopes = (weights * (products - column(2))).astype(BF16)
+        mid_ref[0, :, lanes] = part_ref[0, :, lanes] + diagonal(dot(q_all.T, slopes)).T
+
     each_pair(own_ref.shape[-1], step)
 
 
@@ -217,14 +245,15 @@
     out_ref[1] = tile_order(g_ref[...].astype(F32), odd).astype(BF16)
 
 
-def pack_kernel(odd_ref, own_ref, even_ref, odds_ref, first_ref, second_ref):
-    odd = odd_ref[0] == 1
+def pack_kernel(odd_ref, *refs):
+    odd = odd_ref[0] == 1
+    bands, (first_ref, second_ref) = refs[:-2], refs[-2:]
     for which in range(2):
-        for band, ref in enumerate((own_ref, even_ref, odds_ref)):
+        for at, ref in enumerate(bands):
             x = ref[which].astype(F32).reshape(TILE, 2 * TILE, ref.shape[-1])
             ordered = tile_order(x, odd).astype(BF16)
-            first_ref[which, band * CELLS : (band + 1) * CELLS] = ordered[:CELLS]
-            second_ref[which, band * CELLS : (band + 1) * CELLS] = ordered[CELLS:]
+            first_ref[which, at * CELLS : (at + 1) * CELLS] = ordered[:CELLS]
+            second_ref[which, at * CELLS : (at + 1) * CELLS] = ordered[CELLS:]
 
 
 def finish_kernel(odd_ref, mid_ref, first_ref, second_ref, dk_ref, dv_ref):
@@ -263,35 +292,43 @@
     odd = (lax.axis_index("lon") % 2).astype(jnp.int32)[None]
     field, width = query_field.shape, query_field.shape[-1]
     pairs = width // PAIR
+
+    def named_swap(first, second, axis):
+        second = swap(second, axis, 1, axis == "lon")
+        first = swap(first, axis, 0, axis == "lon")
+        return first, second
+
+    def pack(*bands):
+        column = ((2, len(bands) * CELLS, width), BF16)
+        return call(pack_kernel, [odd], list(bands), [column, column], 1 << 20, 2 << 20)
+
     keys = jnp.stack([key_field.reshape(BAND, width), value_field.reshape(BAND, width)])
-    keys_even = swap(keys, "lat", 0, False)
-    keys_odd = swap(keys, "lat", 1, False)
+    keys_even, keys_odd = named_swap(keys, keys, "lat")
+    first, second = named_swap(*pack(keys, keys_even), "lon")
     (queries,) = call(order_kernel, [odd], [query_field, out_cotangent], [((2, BAND, width), BF16)], 1 << 20, 1 << 20)
-    queries_even = swap(queries, "lat", 0, False)
-    queries_odd = swap(queries, "lat", 1, False)
-    column = ((2, 3 * CELLS, width), BF16)
-    first, second = call(pack_kernel, [odd], [keys, keys_even, keys_odd], [column, column], 1 << 20, 2 << 20)
-    keys_second = swap(second, "lon", 1, True)
-    keys_first = swap(first, "lon", 0, True)
-    around = [queries, keys, keys_even, keys_odd, keys_first, keys_second]
+    queries_even, queries_odd = named_swap(queries, queries, "lat")
+    first_odds, second_odds = named_swap(*pack(keys_odd), "lon")
+    around = [queries, keys, keys_even, keys_odd, first, first_odds, second, second_odds]
     att, stats, low = call(
         attend_kernel, [bias, odd], around,
         [(field, BF16), ((pairs, 8, PAIR), F32), ((pairs, CORE + SIDE, 2 * PAIR), BF16)], 1 << 30, 8 << 20,
     )
-    stats_odd = swap(stats, "lat", 1, False)
-    stats_even = swap(stats, "lat", 0, False)
+    stats_even, stats_odd = named_swap(stats, stats, "lat")
+    tile = ((2, CELLS, width), BF16)
+    to_first, to_second = call(
+        side_kernel, [bias],
+        [first, second, queries, queries_even, queries_odd, stats, stats_even, stats_odd], [tile, tile],
+        1 << 29, 4 << 20,
+    )
+    from_first, from_second = named_swap(to_first, to_second, "lon")
     dq, part = call(
         slope_kernel, [odd], [*around, stats, low],
-        [(field, BF16), ((2, 2 * BAND, width), F32)], 1 << 30, 8 << 20,
-    )
-    tile = ((2, CELLS, width), BF16)
-    mid, first, second = call(
-        key_kernel, [bias],
-        [keys, keys_first, keys_second, queries_even, queries_odd, stats_even, stats_odd, part],
-        [((2, BAND, width), F32), tile, tile], 1 << 30, 8 << 20,
-    )
-    from_second = swap(second, "lon", 1, True)
-    from_first = swap(first, "lon", 0, True)
+        [(field, BF16), ((2, BAND, width), F32)], 1 << 30, 8 << 20,
+    )
+    (mid,) = call(
+        own_kernel, [bias],
+        [keys, queries_even, queries_odd, stats_even, stats_odd, part], [((2, BAND, width), F32)], 1 << 29, 4 << 20,
+    )
     dk, dv = call(
         finish_kernel, [odd], [mid, from_first, from_second], [(field, BF16), (field, BF16)], 1 << 20, 2 << 20
     )

time: 97.5 us -> 111 us (1.14)
  the two profiles are of different devices: /device:TPU:55 before, /device:TPU:63 now
where the time goes in v1:
time: 111 us; the launch traced here: 110 us
  starting transfers between devices  62.1 us (56%)
  waiting for transfers between devices  28.1 us (25%)
  Pallas kernels  18 us (16%)
  other arithmetic  1.11 us (1%)
    ppermute x12, starting transfers between devices, swap(): return lax.ppermute(value, axis, pairs)  62.1 us
    ppermute x12, waiting for transfers between devices, swap(): return lax.ppermute(value, axis, pairs)  28.1 us
    pallas_call x8, Pallas kernels, call(): pl.pallas_call(kernel, in_specs=[pl.BlockSpec(memory_space=pltpu.SMEM)] *...  18 us
  transfers between devices with their start and end apart: 12, of which 4 were waited for; matrix products, arithmetic and copies ran while one was open for 0% of the time, Pallas kernels for 12%

profile of v1, /device:TPU:63, one launch (start us, length us, event | category | flops | bytes accessed | tf_op | source)
XLA Modules:
  0.0 110.1 jit_solution(7339306159014828865)
XLA Ops:
  0.7 1.1 %pad_maximum_fusion.refs_0_.own_ref = bf16[2,128,768]{2,1,0:T(8,128)(2,1)S(1)} fusion(bf16[1,128,768]{2,1,0:T(8,128)(2,1)} %bitcast.4, bf16[1,128,768]{2,1,0:T(8,128)(2,1)} %bitcast.5), kind=kLoop, calls=%fused_computation | loop fusion | flops 196608 | bytes 786432 | tf_op jit(solution)/shard_map/stack | solution.py:305
  1.8 20.2 %collective-permute-start.1 = (bf16[2,128,768]{2,1,0:T(8,128)(2,1)S(1)}, bf16[2,128,768]{2,1,0:T(8,128)(2,1)S(1)}, u32[]{:S(2)}, u32[]{:S(2)}) collective-permute-start(bf16[2,128,768]{2,1,0:T(8,128)(2,1)S(1)} %pad_maximum_fusion.refs_0_.own_ref), channel_id=1, source_target_pairs={{32,64},{64,32},{96,128},{128,96},{160,192},{192,160},{224,256},{2... | collective-permute-start | bytes 1179656 | tf_op jit(solution)/shard_map/ppermute | solution.py:285
  22.0 1.9 %collective-permute-start = (bf16[2,128,768]{2,1,0:T(8,128)(2,1)S(1)}, bf16[2,128,768]{2,1,0:T(8,128)(2,1)S(1)}, u32[]{:S(2)}, u32[]{:S(2)}) collective-permute-start(bf16[2,128,768]{2,1,0:T(8,128)(2,1)S(1)} %pad_maximum_fusion.refs_0_.own_ref), channel_id=1, source_target_pairs={{0,32},{32,0},{64,96},{96,64},{128,160},{160,128},{192,224},{224,1... | collective-permute-start | bytes 1179656 | tf_op jit(solution)/shard_map/ppermute | solution.py:285
  23.9 13.1 %collective-permute-done.1.refs_0_.odds_ref = bf16[2,128,768]{2,1,0:T(8,128)(2,1)S(1)} collective-permute-done((bf16[2,128,768]{2,1,0:T(8,128)(2,1)S(1)}, bf16[2,128,768]{2,1,0:T(8,128)(2,1)S(1)}, u32[]{:S(2)}, u32[]{:S(2)}) %collective-permute-start.1) | collective-permute-done | bytes 393248 | tf_op jit(solution)/shard_map/ppermute | solution.py:285
  37.0 0.7 shard_map.77
  37.7 3.4 %collective-permute-start.3 = (bf16[2,64,768]{2,1,0:T(8,128)(2,1)S(1)}, bf16[2,64,768]{2,1,0:T(8,128)(2,1)S(1)}, u32[]{:S(2)}, u32[]{:S(2)}) collective-permute-start(bf16[2,64,768]{2,1,0:T(8,128)(2,1)S(1)} %get-tuple-element.18), channel_id=1, source_target_pairs={{0,1},{1,0},{2,3},{3,2},{4,5},{5,4},{6,7},{7,6},{8,9},{9,8},{10,11... | collective-permute-start | bytes 589832 | tf_op jit(solution)/shard_map/ppermute | solution.py:285
  41.1 0.0 collective-permute-done.refs_1_.even_ref
  41.2 1.1 shard_map.76
  42.2 1.9 %collective-permute-start.2 = (bf16[2,128,768]{2,1,0:T(8,128)(2,1)}, bf16[2,128,768]{2,1,0:T(8,128)(2,1)S(1)}, u32[]{:S(2)}, u32[]{:S(2)}) collective-permute-start(bf16[2,128,768]{2,1,0:T(8,128)(2,1)} %get-tuple-element.17), channel_id=1, source_target_pairs={{0,1},{1,0},{2,3},{3,2},{4,5},{5,4},{6,7},{7,6},{8,9},{9,8},{10,11... | collective-permute-start | bytes 1179656 | tf_op jit(solution)/shard_map/ppermute | solution.py:285
  44.1 3.8 %collective-permute-start.4 = (bf16[2,128,768]{2,1,0:T(8,128)(2,1)}, bf16[2,128,768]{2,1,0:T(8,128)(2,1)S(1)}, u32[]{:S(2)}, u32[]{:S(2)}) collective-permute-start(bf16[2,128,768]{2,1,0:T(8,128)(2,1)} %get-tuple-element.19), channel_id=1, source_target_pairs={{1,2},{2,1},{3,4},{4,3},{5,6},{6,5},{7,8},{8,7},{9,10},{10,9},{11,... | collective-permute-start | bytes 1179656 | tf_op jit(solution)/shard_map/ppermute | solution.py:285
  48.0 0.1 shard_map.75.mine_ref
  48.1 1.9 %collective-permute-start.6 = (bf16[2,128,768]{2,1,0:T(8,128)(2,1)S(1)}, bf16[2,128,768]{2,1,0:T(8,128)(2,1)S(1)}, u32[]{:S(2)}, u32[]{:S(2)}) collective-permute-start(bf16[2,128,768]{2,1,0:T(8,128)(2,1)S(1)} %shard_map.75.mine_ref), channel_id=1, source_target_pairs={{0,32},{32,0},{64,96},{96,64},{128,160},{160,128},{192,224},{224,1... | collective-permute-start | bytes 1179656 | tf_op jit(solution)/shard_map/ppermute | solution.py:285
  50.0 9.1 %collective-permute-start.7 = (bf16[2,128,768]{2,1,0:T(8,128)(2,1)S(1)}, bf16[2,128,768]{2,1,0:T(8,128)(2,1)S(1)}, u32[]{:S(2)}, u32[]{:S(2)}) collective-permute-start(bf16[2,128,768]{2,1,0:T(8,128)(2,1)S(1)} %shard_map.75.mine_ref), channel_id=1, source_target_pairs={{32,64},{64,32},{96,128},{128,96},{160,192},{192,160},{224,256},{2... | collective-permute-start | bytes 1179656 | tf_op jit(solution)/shard_map/ppermute | solution.py:285
  59.2 0.0 collective-permute-done.3.first_odds_ref
  59.2 6.1 %collective-permute-start.5 = (bf16[2,64,768]{2,1,0:T(8,128)(2,1)}, bf16[2,64,768]{2,1,0:T(8,128)(2,1)S(1)}, u32[]{:S(2)}, u32[]{:S(2)}) collective-permute-start(bf16[2,64,768]{2,1,0:T(8,128)(2,1)} %get-tuple-element.20), channel_id=1, source_target_pairs={{1,2},{2,1},{3,4},{4,3},{5,6},{6,5},{7,8},{8,7},{9,10},{10,9},{11,... | collective-permute-start | bytes 589832 | tf_op jit(solution)/shard_map/ppermute | solution.py:285
  65.3 6.9 %collective-permute-done.5.second_odds_ref = bf16[2,64,768]{2,1,0:T(8,128)(2,1)S(1)} collective-permute-done((bf16[2,64,768]{2,1,0:T(8,128)(2,1)}, bf16[2,64,768]{2,1,0:T(8,128)(2,1)S(1)}, u32[]{:S(2)}, u32[]{:S(2)}) %collective-permute-start.5) | collective-permute-done | bytes 196640 | tf_op jit(solution)/shard_map/ppermute | solution.py:285
  72.2 0.0 collective-permute-done.2.first_ref
  72.2 0.0 collective-permute-done.4.second_ref
  72.2 4.6 %shard_map.78 = (bf16[8,16,768]{2,1,0:T(8,128)(2,1)}, f32[6,8,128]{2,1,0:T(8,128)S(1)}, bf16[6,576,256]{2,1,0:T(8,128)(2,1)S(1)}) custom-call(f32[1]{0:T(128)} %bitcast.bias_ref, s32[1]{0:T(128)} %bitcast.1.odd_ref, bf16[2,128,768]{2,1,0:T(8,128)(2,1)S(1)} %shard_map.75.mine_ref, bf16[2,128,768]{2,1,0:T(8,128)(2,1)S(1)} %pad_maximum_fusion.refs_0_.own_ref, ...), custom_call_target="tpu_custom_call" | custom-call | flops 1073741824 | bytes 8388608 | tf_op jit(solution)/shard_map/pallas_call | solution.py:268
  76.8 1.9 %collective-permute-start.8 = (f32[6,8,128]{2,1,0:T(8,128)S(1)}, f32[6,8,128]{2,1,0:T(8,128)S(1)}, u32[]{:S(2)}, u32[]{:S(2)}) collective-permute-start(f32[6,8,128]{2,1,0:T(8,128)S(1)} %get-tuple-element.22.stats_ref.mine_stats), channel_id=1, source_target_pairs={{0,32},{32,0},{64,96},{96,64},{128,160},{160,128},{192,224},{224,1... | collective-permute-start | bytes 73736 | tf_op jit(solution)/shard_map/ppermute | solution.py:285
  78.7 2.5 %collective-permute-start.9 = (f32[6,8,128]{2,1,0:T(8,128)S(1)}, f32[6,8,128]{2,1,0:T(8,128)S(1)}, u32[]{:S(2)}, u32[]{:S(2)}) collective-permute-start(f32[6,8,128]{2,1,0:T(8,128)S(1)} %get-tuple-element.22.stats_ref.mine_stats), channel_id=1, source_target_pairs={{32,64},{64,32},{96,128},{128,96},{160,192},{192,160},{224,256},{2... | collective-permute-start | bytes 73736 | tf_op jit(solution)/shard_map/ppermute | solution.py:285
  81.2 0.0 collective-permute-done.6.even_ref
  81.2 0.0 collective-permute-done.7.odds_ref
  81.2 0.4 collective-permute-done.8.even_stats
  81.6 7.7 %collective-permute-done.9.odds_stats = f32[6,8,128]{2,1,0:T(8,128)S(1)} collective-permute-done((f32[6,8,128]{2,1,0:T(8,128)S(1)}, f32[6,8,128]{2,1,0:T(8,128)S(1)}, u32[]{:S(2)}, u32[]{:S(2)}) %collective-permute-start.9) | collective-permute-done | bytes 24608 | tf_op jit(solution)/shard_map/ppermute | solution.py:285
  89.3 3.9 %shard_map.81 = (bf16[2,64,768]{2,1,0:T(8,128)(2,1)S(1)}, bf16[2,64,768]{2,1,0:T(8,128)(2,1)S(1)}) custom-call(f32[1]{0:T(128)} %bitcast.bias_ref, bf16[2,128,768]{2,1,0:T(8,128)(2,1)S(1)} %collective-permute-done.2.first_ref, bf16[2,128,768]{2,1,0:T(8,128)(2,1)S(1)} %collective-permute-done.4.second_ref, bf16[2,128,768]{2,1,0:T(8,128)(2,1)S(1)} %shard_map.75.mine_ref, ...), custom_call_target="tpu_custom_call" | custom-call | flops 536870912 | bytes 4194304 | tf_op jit(solution)/shard_map/pallas_call | solution.py:268
  93.2 1.9 %collective-permute-start.10 = (bf16[2,64,768]{2,1,0:T(8,128)(2,1)S(1)}, bf16[2,64,768]{2,1,0:T(8,128)(2,1)S(1)}, u32[]{:S(2)}, u32[]{:S(2)}) collective-permute-start(bf16[2,64,768]{2,1,0:T(8,128)(2,1)S(1)} %get-tuple-element.26), channel_id=1, source_target_pairs={{0,1},{1,0},{2,3},{3,2},{4,5},{5,4},{6,7},{7,6},{8,9},{9,8},{10,11... | collective-permute-start | bytes 589832 | tf_op jit(solution)/shard_map/ppermute | solution.py:285
  95.1 7.4 %collective-permute-start.11 = (bf16[2,64,768]{2,1,0:T(8,128)(2,1)S(1)}, bf16[2,64,768]{2,1,0:T(8,128)(2,1)S(1)}, u32[]{:S(2)}, u32[]{:S(2)}) collective-permute-start(bf16[2,64,768]{2,1,0:T(8,128)(2,1)S(1)} %get-tuple-element.27), channel_id=1, source_target_pairs={{1,2},{2,1},{3,4},{4,3},{5,6},{6,5},{7,8},{8,7},{9,10},{10,9},{11,... | collective-permute-start | bytes 589832 | tf_op jit(solution)/shard_map/ppermute | solution.py:285
  102.5 3.6 %shard_map.79 = (bf16[8,16,768]{2,1,0:T(8,128)(2,1)}, f32[2,128,768]{2,1,0:T(8,128)S(1)}) custom-call(s32[1]{0:T(128)} %bitcast.1.odd_ref, bf16[2,128,768]{2,1,0:T(8,128)(2,1)S(1)} %shard_map.75.mine_ref, bf16[2,128,768]{2,1,0:T(8,128)(2,1)S(1)} %pad_maximum_fusion.refs_0_.own_ref, bf16[2,128,768]{2,1,0:T(8,128)(2,1)S(1)} %collective-permute-done.refs_1_.even_ref, ...), custom_call_target="tpu_custom_call" | custom-call | flops 1073741824 | bytes 8388608 | tf_op jit(solution)/shard_map/pallas_call | solution.py:268
  106.2 3.2 %shard_map.80.mid_ref = f32[2,128,768]{2,1,0:T(8,128)S(1)} custom-call(f32[1]{0:T(128)} %bitcast.bias_ref, bf16[2,128,768]{2,1,0:T(8,128)(2,1)S(1)} %pad_maximum_fusion.refs_0_.own_ref, bf16[2,128,768]{2,1,0:T(8,128)(2,1)S(1)} %collective-permute-done.6.even_ref, bf16[2,128,768]{2,1,0:T(8,128)(2,1)S(1)} %collective-permute-done.7.odds_ref, ...), custom_call_target="tpu_custom_call" | custom-call | flops 536870912 | bytes 4194304 | tf_op jit(solution)/shard_map/pallas_call | solution.py:268
  109.3 0.0 collective-permute-done.10.first_ref
  109.3 0.8 shard_map.82
  (5 shorter events, 0.0 us)
Async XLA Ops:
  0.6 47.3 %copy-start = (bf16[8,16,768]{2,1,0:T(8,128)(2,1)S(1)}, bf16[8,16,768]{2,1,0:T(8,128)(2,1)}, u32[]{:S(2)}) copy-start(bf16[8,16,768]{2,1,0:T(8,128)(2,1)} %q_ref.1) | copy-start | bytes 589828
  0.6 47.3 %copy-start.1 = (bf16[8,16,768]{2,1,0:T(8,128)(2,1)S(1)}, bf16[8,16,768]{2,1,0:T(8,128)(2,1)}, u32[]{:S(2)}) copy-start(bf16[8,16,768]{2,1,0:T(8,128)(2,1)} %g_ref.1) | copy-start | bytes 589828
  1.8 35.2 %collective-permute-start.1 = (bf16[2,128,768]{2,1,0:T(8,128)(2,1)S(1)}, bf16[2,128,768]{2,1,0:T(8,128)(2,1)S(1)}, u32[]{:S(2)}, u32[]{:S(2)}) collective-permute-start(bf16[2,128,768]{2,1,0:T(8,128)(2,1)S(1)} %pad_maximum_fusion.refs_0_.own_ref), channel_id=1, source_target_pairs={{32,64},{64,32},{96,128},{128,96},{160,192},{192,160},{224,256},{2... | collective-permute-start | bytes 1179656 | tf_op jit(solution)/shard_map/ppermute | solution.py:285
  22.0 19.2 %collective-permute-start = (bf16[2,128,768]{2,1,0:T(8,128)(2,1)S(1)}, bf16[2,128,768]{2,1,0:T(8,128)(2,1)S(1)}, u32[]{:S(2)}, u32[]{:S(2)}) collective-permute-start(bf16[2,128,768]{2,1,0:T(8,128)(2,1)S(1)} %pad_maximum_fusion.refs_0_.own_ref), channel_id=1, source_target_pairs={{0,32},{32,0},{64,96},{96,64},{128,160},{160,128},{192,224},{224,1... | collective-permute-start | bytes 1179656 | tf_op jit(solution)/shard_map/ppermute | solution.py:285
  37.7 21.5 %collective-permute-start.3 = (bf16[2,64,768]{2,1,0:T(8,128)(2,1)S(1)}, bf16[2,64,768]{2,1,0:T(8,128)(2,1)S(1)}, u32[]{:S(2)}, u32[]{:S(2)}) collective-permute-start(bf16[2,64,768]{2,1,0:T(8,128)(2,1)S(1)} %get-tuple-element.18), channel_id=1, source_target_pairs={{0,1},{1,0},{2,3},{3,2},{4,5},{5,4},{6,7},{7,6},{8,9},{9,8},{10,11... | collective-permute-start | bytes 589832 | tf_op jit(solution)/shard_map/ppermute | solution.py:285
  42.2 30.0 %collective-permute-start.2 = (bf16[2,128,768]{2,1,0:T(8,128)(2,1)}, bf16[2,128,768]{2,1,0:T(8,128)(2,1)S(1)}, u32[]{:S(2)}, u32[]{:S(2)}) collective-permute-start(bf16[2,128,768]{2,1,0:T(8,128)(2,1)} %get-tuple-element.17), channel_id=1, source_target_pairs={{0,1},{1,0},{2,3},{3,2},{4,5},{5,4},{6,7},{7,6},{8,9},{9,8},{10,11... | collective-permute-start | bytes 1179656 | tf_op jit(solution)/shard_map/ppermute | solution.py:285
  44.1 28.0 %collective-permute-start.4 = (bf16[2,128,768]{2,1,0:T(8,128)(2,1)}, bf16[2,128,768]{2,1,0:T(8,128)(2,1)S(1)}, u32[]{:S(2)}, u32[]{:S(2)}) collective-permute-start(bf16[2,128,768]{2,1,0:T(8,128)(2,1)} %get-tuple-element.19), channel_id=1, source_target_pairs={{1,2},{2,1},{3,4},{4,3},{5,6},{6,5},{7,8},{8,7},{9,10},{10,9},{11,... | collective-permute-start | bytes 1179656 | tf_op jit(solution)/shard_map/ppermute | solution.py:285
  48.1 33.1 %collective-permute-start.6 = (bf16[2,128,768]{2,1,0:T(8,128)(2,1)S(1)}, bf16[2,128,768]{2,1,0:T(8,128)(2,1)S(1)}, u32[]{:S(2)}, u32[]{:S(2)}) collective-permute-start(bf16[2,128,768]{2,1,0:T(8,128)(2,1)S(1)} %shard_map.75.mine_ref), channel_id=1, source_target_pairs={{0,32},{32,0},{64,96},{96,64},{128,160},{160,128},{192,224},{224,1... | collective-permute-start | bytes 1179656 | tf_op jit(solution)/shard_map/ppermute | solution.py:285
  50.0 31.2 %collective-permute-start.7 = (bf16[2,128,768]{2,1,0:T(8,128)(2,1)S(1)}, bf16[2,128,768]{2,1,0:T(8,128)(2,1)S(1)}, u32[]{:S(2)}, u32[]{:S(2)}) collective-permute-start(bf16[2,128,768]{2,1,0:T(8,128)(2,1)S(1)} %shard_map.75.mine_ref), channel_id=1, source_target_pairs={{32,64},{64,32},{96,128},{128,96},{160,192},{192,160},{224,256},{2... | collective-permute-start | bytes 1179656 | tf_op jit(solution)/shard_map/ppermute | solution.py:285
  59.2 13.0 %collective-permute-start.5 = (bf16[2,64,768]{2,1,0:T(8,128)(2,1)}, bf16[2,64,768]{2,1,0:T(8,128)(2,1)S(1)}, u32[]{:S(2)}, u32[]{:S(2)}) collective-permute-start(bf16[2,64,768]{2,1,0:T(8,128)(2,1)} %get-tuple-element.20), channel_id=1, source_target_pairs={{1,2},{2,1},{3,4},{4,3},{5,6},{6,5},{7,8},{8,7},{9,10},{10,9},{11,... | collective-permute-start | bytes 589832 | tf_op jit(solution)/shard_map/ppermute | solution.py:285
  76.8 4.9 %collective-permute-start.8 = (f32[6,8,128]{2,1,0:T(8,128)S(1)}, f32[6,8,128]{2,1,0:T(8,128)S(1)}, u32[]{:S(2)}, u32[]{:S(2)}) collective-permute-start(f32[6,8,128]{2,1,0:T(8,128)S(1)} %get-tuple-element.22.stats_ref.mine_stats), channel_id=1, source_target_pairs={{0,32},{32,0},{64,96},{96,64},{128,160},{160,128},{192,224},{224,1... | collective-permute-start | bytes 73736 | tf_op jit(solution)/shard_map/ppermute | solution.py:285
  78.7 10.6 %collective-permute-start.9 = (f32[6,8,128]{2,1,0:T(8,128)S(1)}, f32[6,8,128]{2,1,0:T(8,128)S(1)}, u32[]{:S(2)}, u32[]{:S(2)}) collective-permute-start(f32[6,8,128]{2,1,0:T(8,128)S(1)} %get-tuple-element.22.stats_ref.mine_stats), channel_id=1, source_target_pairs={{32,64},{64,32},{96,128},{128,96},{160,192},{192,160},{224,256},{2... | collective-permute-start | bytes 73736 | tf_op jit(solution)/shard_map/ppermute | solution.py:285
  93.2 16.1 %collective-permute-start.10 = (bf16[2,64,768]{2,1,0:T(8,128)(2,1)S(1)}, bf16[2,64,768]{2,1,0:T(8,128)(2,1)S(1)}, u32[]{:S(2)}, u32[]{:S(2)}) collective-permute-start(bf16[2,64,768]{2,1,0:T(8,128)(2,1)S(1)} %get-tuple-element.26), channel_id=1, source_target_pairs={{0,1},{1,0},{2,3},{3,2},{4,5},{5,4},{6,7},{7,6},{8,9},{9,8},{10,11... | collective-permute-start | bytes 589832 | tf_op jit(solution)/shard_map/ppermute | solution.py:285
  95.1 14.2 %collective-permute-start.11 = (bf16[2,64,768]{2,1,0:T(8,128)(2,1)S(1)}, bf16[2,64,768]{2,1,0:T(8,128)(2,1)S(1)}, u32[]{:S(2)}, u32[]{:S(2)}) collective-permute-start(bf16[2,64,768]{2,1,0:T(8,128)(2,1)S(1)} %get-tuple-element.27), channel_id=1, source_target_pairs={{1,2},{2,1},{3,4},{4,3},{5,6},{6,5},{7,8},{8,7},{9,10},{10,9},{11,... | collective-permute-start | bytes 589832 | tf_op jit(solution)/shard_map/ppermute | solution.py:285

commit v2 on v0

--- a/solution.py
+++ b/solution.py
@@ -217,14 +217,15 @@
     out_ref[1] = tile_order(g_ref[...].astype(F32), odd).astype(BF16)
 
 
-def pack_kernel(odd_ref, own_ref, even_ref, odds_ref, first_ref, second_ref):
-    odd = odd_ref[0] == 1
+def pack_kernel(odd_ref, *refs):
+    odd = odd_ref[0] == 1
+    bands, (first_ref, second_ref) = refs[:-2], refs[-2:]
     for which in range(2):
-        for band, ref in enumerate((own_ref, even_ref, odds_ref)):
+        for at, ref in enumerate(bands):
             x = ref[which].astype(F32).reshape(TILE, 2 * TILE, ref.shape[-1])
             ordered = tile_order(x, odd).astype(BF16)
-            first_ref[which, band * CELLS : (band + 1) * CELLS] = ordered[:CELLS]
-            second_ref[which, band * CELLS : (band + 1) * CELLS] = ordered[CELLS:]
+            first_ref[which, at * CELLS : (at + 1) * CELLS] = ordered[:CELLS]
+            second_ref[which, at * CELLS : (at + 1) * CELLS] = ordered[CELLS:]
 
 
 def finish_kernel(odd_ref, mid_ref, first_ref, second_ref, dk_ref, dv_ref):
@@ -242,7 +243,7 @@
         + [pl.BlockSpec(memory_space=pltpu.VMEM)] * len(arrays),
         out_specs=[pl.BlockSpec(memory_space=pltpu.VMEM)] * len(outs),
         out_shape=[jax.ShapeDtypeStruct(*out) for out in outs],
-        compiler_params=pltpu.CompilerParams(vmem_limit_bytes=32 << 20),
+        compiler_params=pltpu.CompilerParams(vmem_limit_bytes=20 << 20),
         cost_estimate=pl.CostEstimate(flops=flops, bytes_accessed=moved, transcendentals=0),
     )(*scalars, *arrays)
 
@@ -263,35 +264,38 @@
     odd = (lax.axis_index("lon") % 2).astype(jnp.int32)[None]
     field, width = query_field.shape, query_field.shape[-1]
     pairs = width // PAIR
+
+    def named_swap(first, second, axis):
+        second = swap(second, axis, 1, axis == "lon")
+        first = swap(first, axis, 0, axis == "lon")
+        return first, second
+
+    def pack(*bands):
+        column = ((2, len(bands) * CELLS, width), BF16)
+        return call(pack_kernel, [odd], list(bands), [column, column], 1 << 20, 2 << 20)
+
     keys = jnp.stack([key_field.reshape(BAND, width), value_field.reshape(BAND, width)])
-    keys_even = swap(keys, "lat", 0, False)
-    keys_odd = swap(keys, "lat", 1, False)
+    keys_even, keys_odd = named_swap(keys, keys, "lat")
     (queries,) = call(order_kernel, [odd], [query_field, out_cotangent], [((2, BAND, width), BF16)], 1 << 20, 1 << 20)
-    queries_even = swap(queries, "lat", 0, False)
-    queries_odd = swap(queries, "lat", 1, False)
-    column = ((2, 3 * CELLS, width), BF16)
-    first, second = call(pack_kernel, [odd], [keys, keys_even, keys_odd], [column, column], 1 << 20, 2 << 20)
-    keys_second = swap(second, "lon", 1, True)
-    keys_first = swap(first, "lon", 0, True)
-    around = [queries, keys, keys_even, keys_odd, keys_first, keys_second]
+    queries_even, queries_odd = named_swap(queries, queries, "lat")
+    first, second = named_swap(*pack(keys, keys_even, keys_odd), "lon")
+    around = [queries, keys, keys_even, keys_odd, first, second]
     att, stats, low = call(
         attend_kernel, [bias, odd], around,
         [(field, BF16), ((pairs, 8, PAIR), F32), ((pairs, CORE + SIDE, 2 * PAIR), BF16)], 1 << 30, 8 << 20,
     )
-    stats_odd = swap(stats, "lat", 1, False)
-    stats_even = swap(stats, "lat", 0, False)
+    stats_even, stats_odd = named_swap(stats, stats, "lat")
     dq, part = call(
         slope_kernel, [odd], [*around, stats, low],
         [(field, BF16), ((2, 2 * BAND, width), F32)], 1 << 30, 8 << 20,
     )
     tile = ((2, CELLS, width), BF16)
-    mid, first, second = call(
+    mid, to_first, to_second = call(
         key_kernel, [bias],
-        [keys, keys_first, keys_second, queries_even, queries_odd, stats_even, stats_odd, part],
+        [keys, first, second, queries_even, queries_odd, stats_even, stats_odd, part],
         [((2, BAND, width), F32), tile, tile], 1 << 30, 8 << 20,
     )
-    from_second = swap(second, "lon", 1, True)
-    from_first = swap(first, "lon", 0, True)
+    from_first, from_second = named_swap(to_first, to_second, "lon")
     dk, dv = call(
         finish_kernel, [odd], [mid, from_first, from_second], [(field, BF16), (field, BF16)], 1 << 20, 2 << 20
     )

time: 97.5 us -> 97.5 us (level)
  no operation moved by 1% of the time
where the time goes in v2:
time: 97.5 us; the launch traced here: 97.1 us
  starting transfers between devices  54.2 us (56%)
  waiting for transfers between devices  26.3 us (27%)
  Pallas kernels  14.6 us (15%)
  other arithmetic  1.11 us (1%)
    ppermute x10, starting transfers between devices, swap(): return lax.ppermute(value, axis, pairs)  54.2 us
    ppermute x10, waiting for transfers between devices, swap(): return lax.ppermute(value, axis, pairs)  26.3 us
    pallas_call x6, Pallas kernels, call(): pl.pallas_call(kernel, in_specs=[pl.BlockSpec(memory_space=pltpu.SMEM)] *...  14.6 us
  transfers between devices with their start and end apart: 10, of which 3 were waited for; matrix products, arithmetic and copies ran while one was open for 0% of the time, Pallas kernels for 8%

profile of v2, /device:TPU:55, one launch (start us, length us, event | category | flops | bytes accessed | tf_op | source)
XLA Modules:
  0.0 97.1 jit_solution(8124854831745361208)
XLA Ops:
  0.6 0.0 copy-start
  0.6 0.0 copy-start.1
  0.7 1.1 %pad_maximum_fusion.refs_0_.own_ref = bf16[2,128,768]{2,1,0:T(8,128)(2,1)S(1)} fusion(bf16[1,128,768]{2,1,0:T(8,128)(2,1)} %bitcast.4, bf16[1,128,768]{2,1,0:T(8,128)(2,1)} %bitcast.5), kind=kLoop, calls=%fused_computation | loop fusion | flops 196608 | bytes 786432 | tf_op jit(solution)/shard_map/stack | solution.py:277
  1.8 4.0 %collective-permute-start = (bf16[2,128,768]{2,1,0:T(8,128)(2,1)S(1)}, bf16[2,128,768]{2,1,0:T(8,128)(2,1)S(1)}, u32[]{:S(2)}, u32[]{:S(2)}) collective-permute-start(bf16[2,128,768]{2,1,0:T(8,128)(2,1)S(1)} %pad_maximum_fusion.refs_0_.own_ref), channel_id=1, source_target_pairs={{0,32},{32,0},{64,96},{96,64},{128,160},{160,128},{192,224},{224,1... | collective-permute-start | bytes 1179656 | tf_op jit(solution)/shard_map/ppermute | solution.py:257
  5.8 17.5 %collective-permute-start.1 = (bf16[2,128,768]{2,1,0:T(8,128)(2,1)S(1)}, bf16[2,128,768]{2,1,0:T(8,128)(2,1)S(1)}, u32[]{:S(2)}, u32[]{:S(2)}) collective-permute-start(bf16[2,128,768]{2,1,0:T(8,128)(2,1)S(1)} %pad_maximum_fusion.refs_0_.own_ref), channel_id=1, source_target_pairs={{32,64},{64,32},{96,128},{128,96},{160,192},{192,160},{224,256},{2... | collective-permute-start | bytes 1179656 | tf_op jit(solution)/shard_map/ppermute | solution.py:257
  23.3 0.0 collective-permute-done.refs_1_.even_ref
  23.3 15.8 %collective-permute-done.1.refs_2_.odds_ref = bf16[2,128,768]{2,1,0:T(8,128)(2,1)S(1)} collective-permute-done((bf16[2,128,768]{2,1,0:T(8,128)(2,1)S(1)}, bf16[2,128,768]{2,1,0:T(8,128)(2,1)S(1)}, u32[]{:S(2)}, u32[]{:S(2)}) %collective-permute-start.1) | collective-permute-done | bytes 393248 | tf_op jit(solution)/shard_map/ppermute | solution.py:257
  39.1 1.3 %shard_map.76 = (bf16[2,192,768]{2,1,0:T(8,128)(2,1)}, bf16[2,192,768]{2,1,0:T(8,128)(2,1)}) custom-call(s32[1]{0:T(128)} %bitcast.1.odd_ref, bf16[2,128,768]{2,1,0:T(8,128)(2,1)S(1)} %pad_maximum_fusion.refs_0_.own_ref, bf16[2,128,768]{2,1,0:T(8,128)(2,1)S(1)} %collective-permute-done.refs_1_.even_ref, ...), custom_call_target="tpu_custom_call" | custom-call | flops 1048576 | bytes 2097152 | tf_op jit(solution)/shard_map/pallas_call | solution.py:240
  40.3 4.4 %collective-permute-start.2 = (bf16[2,192,768]{2,1,0:T(8,128)(2,1)}, bf16[2,192,768]{2,1,0:T(8,128)(2,1)S(1)}, u32[]{:S(2)}, u32[]{:S(2)}) collective-permute-start(bf16[2,192,768]{2,1,0:T(8,128)(2,1)} %get-tuple-element.16), channel_id=1, source_target_pairs={{0,1},{1,0},{2,3},{3,2},{4,5},{5,4},{6,7},{7,6},{8,9},{9,8},{10,11... | collective-permute-start | bytes 1769480 | tf_op jit(solution)/shard_map/ppermute | solution.py:257
  44.8 1.9 %collective-permute-start.3 = (bf16[2,192,768]{2,1,0:T(8,128)(2,1)}, bf16[2,192,768]{2,1,0:T(8,128)(2,1)S(1)}, u32[]{:S(2)}, u32[]{:S(2)}) collective-permute-start(bf16[2,192,768]{2,1,0:T(8,128)(2,1)} %get-tuple-element.17), channel_id=1, source_target_pairs={{1,2},{2,1},{3,4},{4,3},{5,6},{6,5},{7,8},{8,7},{9,10},{10,9},{11,... | collective-permute-start | bytes 1769480 | tf_op jit(solution)/shard_map/ppermute | solution.py:257
  46.7 0.0 copy-done
  46.7 0.0 copy-done.1
  46.7 0.1 shard_map.75.mine_ref
  46.8 1.9 %collective-permute-start.4 = (bf16[2,128,768]{2,1,0:T(8,128)(2,1)S(1)}, bf16[2,128,768]{2,1,0:T(8,128)(2,1)S(1)}, u32[]{:S(2)}, u32[]{:S(2)}) collective-permute-start(bf16[2,128,768]{2,1,0:T(8,128)(2,1)S(1)} %shard_map.75.mine_ref), channel_id=1, source_target_pairs={{0,32},{32,0},{64,96},{96,64},{128,160},{160,128},{192,224},{224,1... | collective-permute-start | bytes 1179656 | tf_op jit(solution)/shard_map/ppermute | solution.py:257
  48.8 9.4 %collective-permute-start.5 = (bf16[2,128,768]{2,1,0:T(8,128)(2,1)S(1)}, bf16[2,128,768]{2,1,0:T(8,128)(2,1)S(1)}, u32[]{:S(2)}, u32[]{:S(2)}) collective-permute-start(bf16[2,128,768]{2,1,0:T(8,128)(2,1)S(1)} %shard_map.75.mine_ref), channel_id=1, source_target_pairs={{32,64},{64,32},{96,128},{128,96},{160,192},{192,160},{224,256},{2... | collective-permute-start | bytes 1179656 | tf_op jit(solution)/shard_map/ppermute | solution.py:257
  58.2 0.0 collective-permute-done.2.first_ref
  58.2 3.3 %collective-permute-done.3.second_ref = bf16[2,192,768]{2,1,0:T(8,128)(2,1)S(1)} collective-permute-done((bf16[2,192,768]{2,1,0:T(8,128)(2,1)}, bf16[2,192,768]{2,1,0:T(8,128)(2,1)S(1)}, u32[]{:S(2)}, u32[]{:S(2)}) %collective-permute-start.3) | collective-permute-done | bytes 589856 | tf_op jit(solution)/shard_map/ppermute | solution.py:257
  61.5 4.6 %shard_map.77 = (bf16[8,16,768]{2,1,0:T(8,128)(2,1)}, f32[6,8,128]{2,1,0:T(8,128)S(1)}, bf16[6,576,256]{2,1,0:T(8,128)(2,1)S(1)}) custom-call(f32[1]{0:T(128)} %bitcast.bias_ref, s32[1]{0:T(128)} %bitcast.1.odd_ref, bf16[2,128,768]{2,1,0:T(8,128)(2,1)S(1)} %shard_map.75.mine_ref, bf16[2,128,768]{2,1,0:T(8,128)(2,1)S(1)} %pad_maximum_fusion.refs_0_.own_ref, ...), custom_call_target="tpu_custom_call" | custom-call | flops 1073741824 | bytes 8388608 | tf_op jit(solution)/shard_map/pallas_call | solution.py:240
  66.1 1.9 %collective-permute-start.6 = (f32[6,8,128]{2,1,0:T(8,128)S(1)}, f32[6,8,128]{2,1,0:T(8,128)S(1)}, u32[]{:S(2)}, u32[]{:S(2)}) collective-permute-start(f32[6,8,128]{2,1,0:T(8,128)S(1)} %get-tuple-element.19.stats_ref), channel_id=1, source_target_pairs={{0,32},{32,0},{64,96},{96,64},{128,160},{160,128},{192,224},{224,1... | collective-permute-start | bytes 73736 | tf_op jit(solution)/shard_map/ppermute | solution.py:257
  68.0 9.4 %collective-permute-start.7 = (f32[6,8,128]{2,1,0:T(8,128)S(1)}, f32[6,8,128]{2,1,0:T(8,128)S(1)}, u32[]{:S(2)}, u32[]{:S(2)}) collective-permute-start(f32[6,8,128]{2,1,0:T(8,128)S(1)} %get-tuple-element.19.stats_ref), channel_id=1, source_target_pairs={{32,64},{64,32},{96,128},{128,96},{160,192},{192,160},{224,256},{2... | collective-permute-start | bytes 73736 | tf_op jit(solution)/shard_map/ppermute | solution.py:257
  77.4 3.4 %shard_map.78 = (bf16[8,16,768]{2,1,0:T(8,128)(2,1)}, f32[2,256,768]{2,1,0:T(8,128)S(1)}) custom-call(s32[1]{0:T(128)} %bitcast.1.odd_ref, bf16[2,128,768]{2,1,0:T(8,128)(2,1)S(1)} %shard_map.75.mine_ref, bf16[2,128,768]{2,1,0:T(8,128)(2,1)S(1)} %pad_maximum_fusion.refs_0_.own_ref, bf16[2,128,768]{2,1,0:T(8,128)(2,1)S(1)} %collective-permute-done.refs_1_.even_ref, ...), custom_call_target="tpu_custom_call" | custom-call | flops 1073741824 | bytes 8388608 | tf_op jit(solution)/shard_map/pallas_call | solution.py:240
  80.8 0.0 collective-permute-done.4.even_ref
  80.8 0.0 collective-permute-done.5.odds_ref
  80.8 0.0 collective-permute-done.6.even_stats
  80.8 0.0 collective-permute-done.7.odds_stats
  80.8 4.4 %shard_map.79 = (f32[2,128,768]{2,1,0:T(8,128)S(1)}, bf16[2,64,768]{2,1,0:T(8,128)(2,1)S(1)}, bf16[2,64,768]{2,1,0:T(8,128)(2,1)S(1)}) custom-call(f32[1]{0:T(128)} %bitcast.bias_ref, bf16[2,128,768]{2,1,0:T(8,128)(2,1)S(1)} %pad_maximum_fusion.refs_0_.own_ref, bf16[2,192,768]{2,1,0:T(8,128)(2,1)S(1)} %collective-permute-done.2.first_ref, ...), custom_call_target="tpu_custom_call" | custom-call | flops 1073741824 | bytes 8388608 | tf_op jit(solution)/shard_map/pallas_call | solution.py:240
  85.3 1.9 %collective-permute-start.8 = (bf16[2,64,768]{2,1,0:T(8,128)(2,1)S(1)}, bf16[2,64,768]{2,1,0:T(8,128)(2,1)S(1)}, u32[]{:S(2)}, u32[]{:S(2)}) collective-permute-start(bf16[2,64,768]{2,1,0:T(8,128)(2,1)S(1)} %get-tuple-element.24), channel_id=1, source_target_pairs={{0,1},{1,0},{2,3},{3,2},{4,5},{5,4},{6,7},{7,6},{8,9},{9,8},{10,11... | collective-permute-start | bytes 589832 | tf_op jit(solution)/shard_map/ppermute | solution.py:257
  87.2 1.9 %collective-permute-start.9 = (bf16[2,64,768]{2,1,0:T(8,128)(2,1)S(1)}, bf16[2,64,768]{2,1,0:T(8,128)(2,1)S(1)}, u32[]{:S(2)}, u32[]{:S(2)}) collective-permute-start(bf16[2,64,768]{2,1,0:T(8,128)(2,1)S(1)} %get-tuple-element.25), channel_id=1, source_target_pairs={{1,2},{2,1},{3,4},{4,3},{5,6},{6,5},{7,8},{8,7},{9,10},{10,9},{11,... | collective-permute-start | bytes 589832 | tf_op jit(solution)/shard_map/ppermute | solution.py:257
  89.1 0.0 collective-permute-done.8.first_ref
  89.1 7.2 %collective-permute-done.9.second_ref = bf16[2,64,768]{2,1,0:T(8,128)(2,1)S(1)} collective-permute-done((bf16[2,64,768]{2,1,0:T(8,128)(2,1)S(1)}, bf16[2,64,768]{2,1,0:T(8,128)(2,1)S(1)}, u32[]{:S(2)}, u32[]{:S(2)}) %collective-permute-start.9) | collective-permute-done | bytes 196640 | tf_op jit(solution)/shard_map/ppermute | solution.py:257
  96.3 0.8 shard_map.80
Async XLA Ops:
  0.6 46.1 %copy-start = (bf16[8,16,768]{2,1,0:T(8,128)(2,1)S(1)}, bf16[8,16,768]{2,1,0:T(8,128)(2,1)}, u32[]{:S(2)}) copy-start(bf16[8,16,768]{2,1,0:T(8,128)(2,1)} %q_ref.1) | copy-start | bytes 589828
  0.6 46.1 %copy-start.1 = (bf16[8,16,768]{2,1,0:T(8,128)(2,1)S(1)}, bf16[8,16,768]{2,1,0:T(8,128)(2,1)}, u32[]{:S(2)}) copy-start(bf16[8,16,768]{2,1,0:T(8,128)(2,1)} %g_ref.1) | copy-start | bytes 589828
  1.8 21.5 %collective-permute-start = (bf16[2,128,768]{2,1,0:T(8,128)(2,1)S(1)}, bf16[2,128,768]{2,1,0:T(8,128)(2,1)S(1)}, u32[]{:S(2)}, u32[]{:S(2)}) collective-permute-start(bf16[2,128,768]{2,1,0:T(8,128)(2,1)S(1)} %pad_maximum_fusion.refs_0_.own_ref), channel_id=1, source_target_pairs={{0,32},{32,0},{64,96},{96,64},{128,160},{160,128},{192,224},{224,1... | collective-permute-start | bytes 1179656 | tf_op jit(solution)/shard_map/ppermute | solution.py:257
  5.8 33.3 %collective-permute-start.1 = (bf16[2,128,768]{2,1,0:T(8,128)(2,1)S(1)}, bf16[2,128,768]{2,1,0:T(8,128)(2,1)S(1)}, u32[]{:S(2)}, u32[]{:S(2)}) collective-permute-start(bf16[2,128,768]{2,1,0:T(8,128)(2,1)S(1)} %pad_maximum_fusion.refs_0_.own_ref), channel_id=1, source_target_pairs={{32,64},{64,32},{96,128},{128,96},{160,192},{192,160},{224,256},{2... | collective-permute-start | bytes 1179656 | tf_op jit(solution)/shard_map/ppermute | solution.py:257
  40.3 17.8 %collective-permute-start.2 = (bf16[2,192,768]{2,1,0:T(8,128)(2,1)}, bf16[2,192,768]{2,1,0:T(8,128)(2,1)S(1)}, u32[]{:S(2)}, u32[]{:S(2)}) collective-permute-start(bf16[2,192,768]{2,1,0:T(8,128)(2,1)} %get-tuple-element.16), channel_id=1, source_target_pairs={{0,1},{1,0},{2,3},{3,2},{4,5},{5,4},{6,7},{7,6},{8,9},{9,8},{10,11... | collective-permute-start | bytes 1769480 | tf_op jit(solution)/shard_map/ppermute | solution.py:257
  44.8 16.7 %collective-permute-start.3 = (bf16[2,192,768]{2,1,0:T(8,128)(2,1)}, bf16[2,192,768]{2,1,0:T(8,128)(2,1)S(1)}, u32[]{:S(2)}, u32[]{:S(2)}) collective-permute-start(bf16[2,192,768]{2,1,0:T(8,128)(2,1)} %get-tuple-element.17), channel_id=1, source_target_pairs={{1,2},{2,1},{3,4},{4,3},{5,6},{6,5},{7,8},{8,7},{9,10},{10,9},{11,... | collective-permute-start | bytes 1769480 | tf_op jit(solution)/shard_map/ppermute | solution.py:257
  46.8 34.0 %collective-permute-start.4 = (bf16[2,128,768]{2,1,0:T(8,128)(2,1)S(1)}, bf16[2,128,768]{2,1,0:T(8,128)(2,1)S(1)}, u32[]{:S(2)}, u32[]{:S(2)}) collective-permute-start(bf16[2,128,768]{2,1,0:T(8,128)(2,1)S(1)} %shard_map.75.mine_ref), channel_id=1, source_target_pairs={{0,32},{32,0},{64,96},{96,64},{128,160},{160,128},{192,224},{224,1... | collective-permute-start | bytes 1179656 | tf_op jit(solution)/shard_map/ppermute | solution.py:257
  48.8 32.0 %collective-permute-start.5 = (bf16[2,128,768]{2,1,0:T(8,128)(2,1)S(1)}, bf16[2,128,768]{2,1,0:T(8,128)(2,1)S(1)}, u32[]{:S(2)}, u32[]{:S(2)}) collective-permute-start(bf16[2,128,768]{2,1,0:T(8,128)(2,1)S(1)} %shard_map.75.mine_ref), channel_id=1, source_target_pairs={{32,64},{64,32},{96,128},{128,96},{160,192},{192,160},{224,256},{2... | collective-permute-start | bytes 1179656 | tf_op jit(solution)/shard_map/ppermute | solution.py:257
  66.1 14.7 %collective-permute-start.6 = (f32[6,8,128]{2,1,0:T(8,128)S(1)}, f32[6,8,128]{2,1,0:T(8,128)S(1)}, u32[]{:S(2)}, u32[]{:S(2)}) collective-permute-start(f32[6,8,128]{2,1,0:T(8,128)S(1)} %get-tuple-element.19.stats_ref), channel_id=1, source_target_pairs={{0,32},{32,0},{64,96},{96,64},{128,160},{160,128},{192,224},{224,1... | collective-permute-start | bytes 73736 | tf_op jit(solution)/shard_map/ppermute | solution.py:257
  68.0 12.8 %collective-permute-start.7 = (f32[6,8,128]{2,1,0:T(8,128)S(1)}, f32[6,8,128]{2,1,0:T(8,128)S(1)}, u32[]{:S(2)}, u32[]{:S(2)}) collective-permute-start(f32[6,8,128]{2,1,0:T(8,128)S(1)} %get-tuple-element.19.stats_ref), channel_id=1, source_target_pairs={{32,64},{64,32},{96,128},{128,96},{160,192},{192,160},{224,256},{2... | collective-permute-start | bytes 73736 | tf_op jit(solution)/shard_map/ppermute | solution.py:257
  85.3 3.9 %collective-permute-start.8 = (bf16[2,64,768]{2,1,0:T(8,128)(2,1)S(1)}, bf16[2,64,768]{2,1,0:T(8,128)(2,1)S(1)}, u32[]{:S(2)}, u32[]{:S(2)}) collective-permute-start(bf16[2,64,768]{2,1,0:T(8,128)(2,1)S(1)} %get-tuple-element.24), channel_id=1, source_target_pairs={{0,1},{1,0},{2,3},{3,2},{4,5},{5,4},{6,7},{7,6},{8,9},{9,8},{10,11... | collective-permute-start | bytes 589832 | tf_op jit(solution)/shard_map/ppermute | solution.py:257
  87.2 9.1 %collective-permute-start.9 = (bf16[2,64,768]{2,1,0:T(8,128)(2,1)S(1)}, bf16[2,64,768]{2,1,0:T(8,128)(2,1)S(1)}, u32[]{:S(2)}, u32[]{:S(2)}) collective-permute-start(bf16[2,64,768]{2,1,0:T(8,128)(2,1)S(1)} %get-tuple-element.25), channel_id=1, source_target_pairs={{1,2},{2,1},{3,4},{4,3},{5,6},{6,5},{7,8},{8,7},{9,10},{10,9},{11,... | collective-permute-start | bytes 589832 | tf_op jit(solution)/shard_map/ppermute | solution.py:257

commit v3 on v2

--- a/solution.py
+++ b/solution.py
@@ -81,15 +81,13 @@
     return [jnp.where(first, x, none), jnp.where(first, none, x)]
 
 
-def attend_kernel(
-    bias_ref, odd_ref, mine_ref, own_ref, even_ref, odds_ref, first_ref, second_ref, att_ref, stats_ref, low_ref
-):
-    odd = odd_ref[0] == 1
-    refs = (own_ref, even_ref, odds_ref, first_ref, second_ref)
+def attend_kernel(bias_ref, odd_ref, mine_ref, *refs):
+    odd = odd_ref[0] == 1
+    k_refs, v_refs, (att_ref, stats_ref, low_ref) = refs[:5], refs[5:10], refs[10:]
 
     def step(p, lanes):
-        k_all = jnp.concatenate([ref[0, :, lanes] for ref in refs], axis=0)
-        v_all = jnp.concatenate([ref[1, :, lanes] for ref in refs], axis=0)
+        k_all = jnp.concatenate([ref[:, lanes] for ref in k_refs], axis=0)
+        v_all = jnp.concatenate([ref[:, lanes] for ref in v_refs], axis=0)
         q_turn = mine_ref[0, :, lanes].astype(F32).T
         g_turn = mine_ref[1, :, lanes].astype(F32).T
         scores = near(dot(k_all, wide(q_turn)))
@@ -116,15 +114,13 @@
     each_pair(mine_ref.shape[-1], step)
 
 
-def slope_kernel(
-    odd_ref, mine_ref, own_ref, even_ref, odds_ref, first_ref, second_ref, stats_ref, low_ref, dq_ref, part_ref
-):
-    odd = odd_ref[0] == 1
-    refs = (own_ref, even_ref, odds_ref, first_ref, second_ref)
+def slope_kernel(odd_ref, mine_ref, *refs):
+    odd = odd_ref[0] == 1
+    k_refs, v_refs, (stats_ref, low_ref, dq_ref, part_ref) = refs[:5], refs[5:10], refs[10:]
 
     def step(p, lanes):
-        k_all = jnp.concatenate([ref[0, :, lanes] for ref in refs], axis=0)
-        v_all = jnp.concatenate([ref[1, :, lanes] for ref in refs], axis=0)
+        k_all = jnp.concatenate([ref[:, lanes] for ref in k_refs], axis=0)
+        v_all = jnp.concatenate([ref[:, lanes] for ref in v_refs], axis=0)
         q_mine, g_mine = mine_ref[0, :, lanes], mine_ref[1, :, lanes]
         stats = stats_ref[p]
         drift = jnp.concatenate([stats[2:3], stats[3:4]], axis=1)
@@ -144,9 +140,10 @@
 
 
 def key_kernel(
-    bias_ref, own_ref, first_ref, second_ref, even_ref, odds_ref, even_stats, odds_stats, part_ref,
-    mid_ref, to_first_ref, to_second_ref,
+    bias_ref, own_k_ref, first_k_ref, second_k_ref, own_v_ref, first_v_ref, second_v_ref,
+    even_ref, odds_ref, even_stats, odds_stats, part_ref, mid_ref, to_first_ref, to_second_ref,
 ):
+    own_refs, first_refs, second_refs = (own_k_ref, own_v_ref), (first_k_ref, first_v_ref), (second_k_ref, second_v_ref)
     refs = (even_ref, odds_ref)
 
     def step(p, lanes):
@@ -154,9 +151,9 @@
         low_row = below((PAIR, PAIR), 0, HEAD_DIM)
 
         def keys(which):
-            own = own_ref[which, :, lanes].astype(F32).T
+            own = own_refs[which][:, lanes].astype(F32).T
             both = jnp.concatenate(
-                [first_ref[which, :CELLS, lanes], second_ref[which, :CELLS, lanes]], axis=0
+                [first_refs[which][:CELLS, lanes], second_refs[which][:CELLS, lanes]], axis=0
             ).astype(F32).T
             turned = pltpu.roll(both, CELLS, axis=1)
             block = low_row == low_lane
@@ -208,7 +205,7 @@
         slopes = weights * (beside(dot(g_all, keys(1))) - column(2))
         store(0, dot(q_all.T, spread(slopes)))
 
-    each_pair(own_ref.shape[-1], step)
+    each_pair(own_k_ref.shape[-1], step)
 
 
 def order_kernel(odd_ref, q_ref, g_ref, out_ref):
@@ -220,12 +217,11 @@
 def pack_kernel(odd_ref, *refs):
     odd = odd_ref[0] == 1
     bands, (first_ref, second_ref) = refs[:-2], refs[-2:]
-    for which in range(2):
-        for at, ref in enumerate(bands):
-            x = ref[which].astype(F32).reshape(TILE, 2 * TILE, ref.shape[-1])
-            ordered = tile_order(x, odd).astype(BF16)
-            first_ref[which, at * CELLS : (at + 1) * CELLS] = ordered[:CELLS]
-            second_ref[which, at * CELLS : (at + 1) * CELLS] = ordered[CELLS:]
+    for at, ref in enumerate(bands):
+        x = ref[...].astype(F32).reshape(TILE, 2 * TILE, ref.shape[-1])
+        ordered = tile_order(x, odd).astype(BF16)
+        first_ref[at * CELLS : (at + 1) * CELLS] = ordered[:CELLS]
+        second_ref[at * CELLS : (at + 1) * CELLS] = ordered[CELLS:]
 
 
 def finish_kernel(odd_ref, mid_ref, first_ref, second_ref, dk_ref, dv_ref):
@@ -271,15 +267,18 @@
         return first, second
 
     def pack(*bands):
-        column = ((2, len(bands) * CELLS, width), BF16)
+        column = ((len(bands) * CELLS, width), BF16)
         return call(pack_kernel, [odd], list(bands), [column, column], 1 << 20, 2 << 20)
 
-    keys = jnp.stack([key_field.reshape(BAND, width), value_field.reshape(BAND, width)])
+    keys, values = key_field.reshape(BAND, width), value_field.reshape(BAND, width)
     keys_even, keys_odd = named_swap(keys, keys, "lat")
+    values_even, values_odd = named_swap(values, values, "lat")
     (queries,) = call(order_kernel, [odd], [query_field, out_cotangent], [((2, BAND, width), BF16)], 1 << 20, 1 << 20)
     queries_even, queries_odd = named_swap(queries, queries, "lat")
-    first, second = named_swap(*pack(keys, keys_even, keys_odd), "lon")
-    around = [queries, keys, keys_even, keys_odd, first, second]
+    first_k, second_k = named_swap(*pack(keys, keys_even, keys_odd), "lon")
+    first_v, second_v = named_swap(*pack(values, values_even, values_odd), "lon")
+    around = [queries, keys, keys_even, keys_odd, first_k, second_k]
+    around += [values, values_even, values_odd, first_v, second_v]
     att, stats, low = call(
         attend_kernel, [bias, odd], around,
         [(field, BF16), ((pairs, 8, PAIR), F32), ((pairs, CORE + SIDE, 2 * PAIR), BF16)], 1 << 30, 8 << 20,
@@ -292,7 +291,7 @@
     tile = ((2, CELLS, width), BF16)
     mid, to_first, to_second = call(
         key_kernel, [bias],
-        [keys, first, second, queries_even, queries_odd, stats_even, stats_odd, part],
+        [keys, first_k, second_k, values, first_v, second_v, queries_even, queries_odd, stats_even, stats_odd, part],
         [((2, BAND, width), F32), tile, tile], 1 << 30, 8 << 20,
     )
     from_first, from_second = named_swap(to_first, to_second, "lon")

time: 97.5 us -> 100 us (1.026)
  the two profiles are of different devices: /device:TPU:55 before, /device:TPU:32 now
where the time goes in v3:
time: 100 us; the launch traced here: 99.5 us
  starting transfers between devices  63.7 us (64%)
  waiting for transfers between devices  16.2 us (16%)
  Pallas kernels  15.1 us (15%)
  local copies, waits for them, and re-layouts  3.71 us (4%)
    ppermute x14, starting transfers between devices, swap(): return lax.ppermute(value, axis, pairs)  63.7 us
    ppermute x14, waiting for transfers between devices, swap(): return lax.ppermute(value, axis, pairs)  16.2 us
    pallas_call x7, Pallas kernels, call(): pl.pallas_call(kernel, in_specs=[pl.BlockSpec(memory_space=pltpu.SMEM)] *...  15.1 us
    unnamed x12, local copies, waits for them, and re-layouts  3.71 us
  transfers between devices with their start and end apart: 14, of which 5 were waited for; matrix products, arithmetic and copies ran while one was open for 0% of the time, Pallas kernels for 10%

profile of v3, /device:TPU:32, one launch (start us, length us, event | category | flops | bytes accessed | tf_op | source)
XLA Modules:
  0.0 99.5 jit_solution(1151994690500725992)
XLA Ops:
  0.6 4.3 %collective-permute-start = (bf16[128,768]{1,0:T(8,128)(2,1)}, bf16[128,768]{1,0:T(8,128)(2,1)S(1)}, u32[]{:S(2)}, u32[]{:S(2)}) collective-permute-start(bf16[128,768]{1,0:T(8,128)(2,1)} %bitcast.4), channel_id=1, source_target_pairs={{0,32},{32,0},{64,96},{96,64},{128,160},{160,128},{192,224},{224,1... | collective-permute-start | bytes 589832 | tf_op jit(solution)/shard_map/ppermute | solution.py:253
  4.9 15.9 %collective-permute-start.1 = (bf16[128,768]{1,0:T(8,128)(2,1)}, bf16[128,768]{1,0:T(8,128)(2,1)S(1)}, u32[]{:S(2)}, u32[]{:S(2)}) collective-permute-start(bf16[128,768]{1,0:T(8,128)(2,1)} %bitcast.5), channel_id=1, source_target_pairs={{32,64},{64,32},{96,128},{128,96},{160,192},{192,160},{224,256},{2... | collective-permute-start | bytes 589832 | tf_op jit(solution)/shard_map/ppermute | solution.py:253
  20.9 1.9 %collective-permute-start.4 = (bf16[128,768]{1,0:T(8,128)(2,1)}, bf16[128,768]{1,0:T(8,128)(2,1)S(1)}, u32[]{:S(2)}, u32[]{:S(2)}) collective-permute-start(bf16[128,768]{1,0:T(8,128)(2,1)} %bitcast.10), channel_id=1, source_target_pairs={{0,32},{32,0},{64,96},{96,64},{128,160},{160,128},{192,224},{224,1... | collective-permute-start | bytes 589832 | tf_op jit(solution)/shard_map/ppermute | solution.py:253
  22.8 3.4 %collective-permute-start.5 = (bf16[128,768]{1,0:T(8,128)(2,1)}, bf16[128,768]{1,0:T(8,128)(2,1)S(1)}, u32[]{:S(2)}, u32[]{:S(2)}) collective-permute-start(bf16[128,768]{1,0:T(8,128)(2,1)} %bitcast.11), channel_id=1, source_target_pairs={{32,64},{64,32},{96,128},{128,96},{160,192},{192,160},{224,256},{2... | collective-permute-start | bytes 589832 | tf_op jit(solution)/shard_map/ppermute | solution.py:253
  26.2 3.5 %collective-permute-done.1.refs_2_ = bf16[128,768]{1,0:T(8,128)(2,1)S(1)} collective-permute-done((bf16[128,768]{1,0:T(8,128)(2,1)}, bf16[128,768]{1,0:T(8,128)(2,1)S(1)}, u32[]{:S(2)}, u32[]{:S(2)}) %collective-permute-start.1) | collective-permute-done | bytes 196640 | tf_op jit(solution)/shard_map/ppermute | solution.py:253
  29.7 0.9 copy-done
  30.7 0.8 shard_map.76
  31.5 1.9 %collective-permute-start.2 = (bf16[192,768]{1,0:T(8,128)(2,1)S(1)}, bf16[192,768]{1,0:T(8,128)(2,1)S(1)}, u32[]{:S(2)}, u32[]{:S(2)}) collective-permute-start(bf16[192,768]{1,0:T(8,128)(2,1)S(1)} %get-tuple-element.18), channel_id=1, source_target_pairs={{0,1},{1,0},{2,3},{3,2},{4,5},{5,4},{6,7},{7,6},{8,9},{9,8},{10,11... | collective-permute-start | bytes 884744 | tf_op jit(solution)/shard_map/ppermute | solution.py:253
  33.4 6.0 %collective-permute-start.3 = (bf16[192,768]{1,0:T(8,128)(2,1)}, bf16[192,768]{1,0:T(8,128)(2,1)S(1)}, u32[]{:S(2)}, u32[]{:S(2)}) collective-permute-start(bf16[192,768]{1,0:T(8,128)(2,1)} %get-tuple-element.19), channel_id=1, source_target_pairs={{1,2},{2,1},{3,4},{4,3},{5,6},{6,5},{7,8},{8,7},{9,10},{10,9},{11,... | collective-permute-start | bytes 884744 | tf_op jit(solution)/shard_map/ppermute | solution.py:253
  39.3 0.0 collective-permute-done.4.refs_1_.refs_6_
  39.3 1.9 %collective-permute-done.5.refs_2_.refs_7_ = bf16[128,768]{1,0:T(8,128)(2,1)S(1)} collective-permute-done((bf16[128,768]{1,0:T(8,128)(2,1)}, bf16[128,768]{1,0:T(8,128)(2,1)S(1)}, u32[]{:S(2)}, u32[]{:S(2)}) %collective-permute-start.5) | collective-permute-done | bytes 196640 | tf_op jit(solution)/shard_map/ppermute | solution.py:253
  41.3 0.9 copy-done.2
  42.2 0.9 shard_map.77
  43.1 1.9 %collective-permute-start.6 = (bf16[192,768]{1,0:T(8,128)(2,1)}, bf16[192,768]{1,0:T(8,128)(2,1)S(1)}, u32[]{:S(2)}, u32[]{:S(2)}) collective-permute-start(bf16[192,768]{1,0:T(8,128)(2,1)} %get-tuple-element.20), channel_id=1, source_target_pairs={{0,1},{1,0},{2,3},{3,2},{4,5},{5,4},{6,7},{7,6},{8,9},{9,8},{10,11... | collective-permute-start | bytes 884744 | tf_op jit(solution)/shard_map/ppermute | solution.py:253
  45.1 6.9 %collective-permute-start.7 = (bf16[192,768]{1,0:T(8,128)(2,1)}, bf16[192,768]{1,0:T(8,128)(2,1)S(1)}, u32[]{:S(2)}, u32[]{:S(2)}) collective-permute-start(bf16[192,768]{1,0:T(8,128)(2,1)} %get-tuple-element.21), channel_id=1, source_target_pairs={{1,2},{2,1},{3,4},{4,3},{5,6},{6,5},{7,8},{8,7},{9,10},{10,9},{11,... | collective-permute-start | bytes 884744 | tf_op jit(solution)/shard_map/ppermute | solution.py:253
  52.0 0.0 copy-start.4
  52.0 0.9 copy-done.4
  52.9 0.9 copy-done.5
  53.8 0.1 shard_map.75.mine_ref
  53.9 1.9 %collective-permute-start.8 = (bf16[2,128,768]{2,1,0:T(8,128)(2,1)S(1)}, bf16[2,128,768]{2,1,0:T(8,128)(2,1)S(1)}, u32[]{:S(2)}, u32[]{:S(2)}) collective-permute-start(bf16[2,128,768]{2,1,0:T(8,128)(2,1)S(1)} %shard_map.75.mine_ref), channel_id=1, source_target_pairs={{0,32},{32,0},{64,96},{96,64},{128,160},{160,128},{192,224},{224,1... | collective-permute-start | bytes 1179656 | tf_op jit(solution)/shard_map/ppermute | solution.py:253
  55.9 5.7 %collective-permute-start.9 = (bf16[2,128,768]{2,1,0:T(8,128)(2,1)S(1)}, bf16[2,128,768]{2,1,0:T(8,128)(2,1)S(1)}, u32[]{:S(2)}, u32[]{:S(2)}) collective-permute-start(bf16[2,128,768]{2,1,0:T(8,128)(2,1)S(1)} %shard_map.75.mine_ref), channel_id=1, source_target_pairs={{32,64},{64,32},{96,128},{128,96},{160,192},{192,160},{224,256},{2... | collective-permute-start | bytes 1179656 | tf_op jit(solution)/shard_map/ppermute | solution.py:253
  61.6 4.6 %shard_map.78 = (bf16[8,16,768]{2,1,0:T(8,128)(2,1)}, f32[6,8,128]{2,1,0:T(8,128)S(1)}, bf16[6,576,256]{2,1,0:T(8,128)(2,1)S(1)}) custom-call(f32[1]{0:T(128)} %bitcast.bias_ref, s32[1]{0:T(128)} %bitcast.1.odd_ref, bf16[2,128,768]{2,1,0:T(8,128)(2,1)S(1)} %shard_map.75.mine_ref, bf16[128,768]{1,0:T(8,128)(2,1)S(1)} %bitcast.7, ...), custom_call_target="tpu_custom_call" | custom-call | flops 1073741824 | bytes 8388608 | tf_op jit(solution)/shard_map/pallas_call | solution.py:236
  66.2 1.9 %collective-permute-start.10 = (f32[6,8,128]{2,1,0:T(8,128)S(1)}, f32[6,8,128]{2,1,0:T(8,128)S(1)}, u32[]{:S(2)}, u32[]{:S(2)}) collective-permute-start(f32[6,8,128]{2,1,0:T(8,128)S(1)} %get-tuple-element.23.refs_10_), channel_id=1, source_target_pairs={{0,32},{32,0},{64,96},{96,64},{128,160},{160,128},{192,224},{224,1... | collective-permute-start | bytes 73736 | tf_op jit(solution)/shard_map/ppermute | solution.py:253
  68.1 6.2 %collective-permute-start.11 = (f32[6,8,128]{2,1,0:T(8,128)S(1)}, f32[6,8,128]{2,1,0:T(8,128)S(1)}, u32[]{:S(2)}, u32[]{:S(2)}) collective-permute-start(f32[6,8,128]{2,1,0:T(8,128)S(1)} %get-tuple-element.23.refs_10_), channel_id=1, source_target_pairs={{32,64},{64,32},{96,128},{128,96},{160,192},{192,160},{224,256},{2... | collective-permute-start | bytes 73736 | tf_op jit(solution)/shard_map/ppermute | solution.py:253
  74.3 3.4 %shard_map.79 = (bf16[8,16,768]{2,1,0:T(8,128)(2,1)}, f32[2,256,768]{2,1,0:T(8,128)S(1)}) custom-call(s32[1]{0:T(128)} %bitcast.1.odd_ref, bf16[2,128,768]{2,1,0:T(8,128)(2,1)S(1)} %shard_map.75.mine_ref, bf16[128,768]{1,0:T(8,128)(2,1)S(1)} %bitcast.8, bf16[128,768]{1,0:T(8,128)(2,1)S(1)} %collective-permute-done.refs_1_, ...), custom_call_target="tpu_custom_call" | custom-call | flops 1073741824 | bytes 8388608 | tf_op jit(solution)/shard_map/pallas_call | solution.py:236
  77.8 1.7 %collective-permute-done.9.odds_ref = bf16[2,128,768]{2,1,0:T(8,128)(2,1)S(1)} collective-permute-done((bf16[2,128,768]{2,1,0:T(8,128)(2,1)S(1)}, bf16[2,128,768]{2,1,0:T(8,128)(2,1)S(1)}, u32[]{:S(2)}, u32[]{:S(2)}) %collective-permute-start.9) | collective-permute-done | bytes 393248 | tf_op jit(solution)/shard_map/ppermute | solution.py:253
  79.5 2.0 %collective-permute-done.11.odds_stats = f32[6,8,128]{2,1,0:T(8,128)S(1)} collective-permute-done((f32[6,8,128]{2,1,0:T(8,128)S(1)}, f32[6,8,128]{2,1,0:T(8,128)S(1)}, u32[]{:S(2)}, u32[]{:S(2)}) %collective-permute-start.11) | collective-permute-done | bytes 24608 | tf_op jit(solution)/shard_map/ppermute | solution.py:253
  81.5 4.4 %shard_map.80 = (f32[2,128,768]{2,1,0:T(8,128)S(1)}, bf16[2,64,768]{2,1,0:T(8,128)(2,1)S(1)}, bf16[2,64,768]{2,1,0:T(8,128)(2,1)S(1)}) custom-call(f32[1]{0:T(128)} %bitcast.bias_ref, bf16[128,768]{1,0:T(8,128)(2,1)S(1)} %bitcast.9, bf16[192,768]{1,0:T(8,128)(2,1)S(1)} %collective-permute-done.2.refs_3_.first_k_ref, ...), custom_call_target="tpu_custom_call" | custom-call | flops 1073741824 | bytes 8388608 | tf_op jit(solution)/shard_map/pallas_call | solution.py:236
  85.9 1.9 %collective-permute-start.12 = (bf16[2,64,768]{2,1,0:T(8,128)(2,1)S(1)}, bf16[2,64,768]{2,1,0:T(8,128)(2,1)S(1)}, u32[]{:S(2)}, u32[]{:S(2)}) collective-permute-start(bf16[2,64,768]{2,1,0:T(8,128)(2,1)S(1)} %get-tuple-element.28), channel_id=1, source_target_pairs={{0,1},{1,0},{2,3},{3,2},{4,5},{5,4},{6,7},{7,6},{8,9},{9,8},{10,11... | collective-permute-start | bytes 589832 | tf_op jit(solution)/shard_map/ppermute | solution.py:253
  87.8 3.8 %collective-permute-start.13 = (bf16[2,64,768]{2,1,0:T(8,128)(2,1)S(1)}, bf16[2,64,768]{2,1,0:T(8,128)(2,1)S(1)}, u32[]{:S(2)}, u32[]{:S(2)}) collective-permute-start(bf16[2,64,768]{2,1,0:T(8,128)(2,1)S(1)} %get-tuple-element.29), channel_id=1, source_target_pairs={{1,2},{2,1},{3,4},{4,3},{5,6},{6,5},{7,8},{8,7},{9,10},{10,9},{11,... | collective-permute-start | bytes 589832 | tf_op jit(solution)/shard_map/ppermute | solution.py:253
  91.7 7.0 %collective-permute-done.13.second_ref = bf16[2,64,768]{2,1,0:T(8,128)(2,1)S(1)} collective-permute-done((bf16[2,64,768]{2,1,0:T(8,128)(2,1)S(1)}, bf16[2,64,768]{2,1,0:T(8,128)(2,1)S(1)}, u32[]{:S(2)}, u32[]{:S(2)}) %collective-permute-start.13) | collective-permute-done | bytes 196640 | tf_op jit(solution)/shard_map/ppermute | solution.py:253
  98.7 0.8 shard_map.81
  (15 shorter events, 0.0 us)
Async XLA Ops:
  0.6 25.6 %collective-permute-start = (bf16[128,768]{1,0:T(8,128)(2,1)}, bf16[128,768]{1,0:T(8,128)(2,1)S(1)}, u32[]{:S(2)}, u32[]{:S(2)}) collective-permute-start(bf16[128,768]{1,0:T(8,128)(2,1)} %bitcast.4), channel_id=1, source_target_pairs={{0,32},{32,0},{64,96},{96,64},{128,160},{160,128},{192,224},{224,1... | collective-permute-start | bytes 589832 | tf_op jit(solution)/shard_map/ppermute | solution.py:253
  4.9 24.8 %collective-permute-start.1 = (bf16[128,768]{1,0:T(8,128)(2,1)}, bf16[128,768]{1,0:T(8,128)(2,1)S(1)}, u32[]{:S(2)}, u32[]{:S(2)}) collective-permute-start(bf16[128,768]{1,0:T(8,128)(2,1)} %bitcast.5), channel_id=1, source_target_pairs={{32,64},{64,32},{96,128},{128,96},{160,192},{192,160},{224,256},{2... | collective-permute-start | bytes 589832 | tf_op jit(solution)/shard_map/ppermute | solution.py:253
  20.9 18.5 %collective-permute-start.4 = (bf16[128,768]{1,0:T(8,128)(2,1)}, bf16[128,768]{1,0:T(8,128)(2,1)S(1)}, u32[]{:S(2)}, u32[]{:S(2)}) collective-permute-start(bf16[128,768]{1,0:T(8,128)(2,1)} %bitcast.10), channel_id=1, source_target_pairs={{0,32},{32,0},{64,96},{96,64},{128,160},{160,128},{192,224},{224,1... | collective-permute-start | bytes 589832 | tf_op jit(solution)/shard_map/ppermute | solution.py:253
  22.8 18.5 %collective-permute-start.5 = (bf16[128,768]{1,0:T(8,128)(2,1)}, bf16[128,768]{1,0:T(8,128)(2,1)S(1)}, u32[]{:S(2)}, u32[]{:S(2)}) collective-permute-start(bf16[128,768]{1,0:T(8,128)(2,1)} %bitcast.11), channel_id=1, source_target_pairs={{32,64},{64,32},{96,128},{128,96},{160,192},{192,160},{224,256},{2... | collective-permute-start | bytes 589832 | tf_op jit(solution)/shard_map/ppermute | solution.py:253
  29.7 0.9 copy-start
  30.7 31.0 %copy-start.1 = (bf16[8,16,768]{2,1,0:T(8,128)(2,1)S(1)}, bf16[8,16,768]{2,1,0:T(8,128)(2,1)}, u32[]{:S(2)}) copy-start(bf16[8,16,768]{2,1,0:T(8,128)(2,1)} %param.5) | copy-start | bytes 589828
  30.7 31.0 %copy-start.3 = (bf16[8,16,768]{2,1,0:T(8,128)(2,1)S(1)}, bf16[8,16,768]{2,1,0:T(8,128)(2,1)}, u32[]{:S(2)}) copy-start(bf16[8,16,768]{2,1,0:T(8,128)(2,1)} %param.6) | copy-start | bytes 589828
  31.5 24.4 %collective-permute-start.2 = (bf16[192,768]{1,0:T(8,128)(2,1)S(1)}, bf16[192,768]{1,0:T(8,128)(2,1)S(1)}, u32[]{:S(2)}, u32[]{:S(2)}) collective-permute-start(bf16[192,768]{1,0:T(8,128)(2,1)S(1)} %get-tuple-element.18), channel_id=1, source_target_pairs={{0,1},{1,0},{2,3},{3,2},{4,5},{5,4},{6,7},{7,6},{8,9},{9,8},{10,11... | collective-permute-start | bytes 884744 | tf_op jit(solution)/shard_map/ppermute | solution.py:253
  33.4 28.2 %collective-permute-start.3 = (bf16[192,768]{1,0:T(8,128)(2,1)}, bf16[192,768]{1,0:T(8,128)(2,1)S(1)}, u32[]{:S(2)}, u32[]{:S(2)}) collective-permute-start(bf16[192,768]{1,0:T(8,128)(2,1)} %get-tuple-element.19), channel_id=1, source_target_pairs={{1,2},{2,1},{3,4},{4,3},{5,6},{6,5},{7,8},{8,7},{9,10},{10,9},{11,... | collective-permute-start | bytes 884744 | tf_op jit(solution)/shard_map/ppermute | solution.py:253
  41.3 0.9 copy-start.2
  43.1 18.5 %collective-permute-start.6 = (bf16[192,768]{1,0:T(8,128)(2,1)}, bf16[192,768]{1,0:T(8,128)(2,1)S(1)}, u32[]{:S(2)}, u32[]{:S(2)}) collective-permute-start(bf16[192,768]{1,0:T(8,128)(2,1)} %get-tuple-element.20), channel_id=1, source_target_pairs={{0,1},{1,0},{2,3},{3,2},{4,5},{5,4},{6,7},{7,6},{8,9},{9,8},{10,11... | collective-permute-start | bytes 884744 | tf_op jit(solution)/shard_map/ppermute | solution.py:253
  45.1 16.5 %collective-permute-start.7 = (bf16[192,768]{1,0:T(8,128)(2,1)}, bf16[192,768]{1,0:T(8,128)(2,1)S(1)}, u32[]{:S(2)}, u32[]{:S(2)}) collective-permute-start(bf16[192,768]{1,0:T(8,128)(2,1)} %get-tuple-element.21), channel_id=1, source_target_pairs={{1,2},{2,1},{3,4},{4,3},{5,6},{6,5},{7,8},{8,7},{9,10},{10,9},{11,... | collective-permute-start | bytes 884744 | tf_op jit(solution)/shard_map/ppermute | solution.py:253
  52.0 0.9 copy-start.4
  52.9 0.9 copy-start.5
  53.9 23.8 %collective-permute-start.8 = (bf16[2,128,768]{2,1,0:T(8,128)(2,1)S(1)}, bf16[2,128,768]{2,1,0:T(8,128)(2,1)S(1)}, u32[]{:S(2)}, u32[]{:S(2)}) collective-permute-start(bf16[2,128,768]{2,1,0:T(8,128)(2,1)S(1)} %shard_map.75.mine_ref), channel_id=1, source_target_pairs={{0,32},{32,0},{64,96},{96,64},{128,160},{160,128},{192,224},{224,1... | collective-permute-start | bytes 1179656 | tf_op jit(solution)/shard_map/ppermute | solution.py:253
  55.9 23.6 %collective-permute-start.9 = (bf16[2,128,768]{2,1,0:T(8,128)(2,1)S(1)}, bf16[2,128,768]{2,1,0:T(8,128)(2,1)S(1)}, u32[]{:S(2)}, u32[]{:S(2)}) collective-permute-start(bf16[2,128,768]{2,1,0:T(8,128)(2,1)S(1)} %shard_map.75.mine_ref), channel_id=1, source_target_pairs={{32,64},{64,32},{96,128},{128,96},{160,192},{192,160},{224,256},{2... | collective-permute-start | bytes 1179656 | tf_op jit(solution)/shard_map/ppermute | solution.py:253
  66.2 13.2 %collective-permute-start.10 = (f32[6,8,128]{2,1,0:T(8,128)S(1)}, f32[6,8,128]{2,1,0:T(8,128)S(1)}, u32[]{:S(2)}, u32[]{:S(2)}) collective-permute-start(f32[6,8,128]{2,1,0:T(8,128)S(1)} %get-tuple-element.23.refs_10_), channel_id=1, source_target_pairs={{0,32},{32,0},{64,96},{96,64},{128,160},{160,128},{192,224},{224,1... | collective-permute-start | bytes 73736 | tf_op jit(solution)/shard_map/ppermute | solution.py:253
  68.1 13.3 %collective-permute-start.11 = (f32[6,8,128]{2,1,0:T(8,128)S(1)}, f32[6,8,128]{2,1,0:T(8,128)S(1)}, u32[]{:S(2)}, u32[]{:S(2)}) collective-permute-start(f32[6,8,128]{2,1,0:T(8,128)S(1)} %get-tuple-element.23.refs_10_), channel_id=1, source_target_pairs={{32,64},{64,32},{96,128},{128,96},{160,192},{192,160},{224,256},{2... | collective-permute-start | bytes 73736 | tf_op jit(solution)/shard_map/ppermute | solution.py:253
  85.9 5.8 %collective-permute-start.12 = (bf16[2,64,768]{2,1,0:T(8,128)(2,1)S(1)}, bf16[2,64,768]{2,1,0:T(8,128)(2,1)S(1)}, u32[]{:S(2)}, u32[]{:S(2)}) collective-permute-start(bf16[2,64,768]{2,1,0:T(8,128)(2,1)S(1)} %get-tuple-element.28), channel_id=1, source_target_pairs={{0,1},{1,0},{2,3},{3,2},{4,5},{5,4},{6,7},{7,6},{8,9},{9,8},{10,11... | collective-permute-start | bytes 589832 | tf_op jit(solution)/shard_map/ppermute | solution.py:253
  87.8 10.9 %collective-permute-start.13 = (bf16[2,64,768]{2,1,0:T(8,128)(2,1)S(1)}, bf16[2,64,768]{2,1,0:T(8,128)(2,1)S(1)}, u32[]{:S(2)}, u32[]{:S(2)}) collective-permute-start(bf16[2,64,768]{2,1,0:T(8,128)(2,1)S(1)} %get-tuple-element.29), channel_id=1, source_target_pairs={{1,2},{2,1},{3,4},{4,3},{5,6},{6,5},{7,8},{8,7},{9,10},{10,9},{11,... | collective-permute-start | bytes 589832 | tf_op jit(solution)/shard_map/ppermute | solution.py:253

commit v4 on v2

--- a/solution.py
+++ b/solution.py
@@ -228,6 +228,18 @@
             second_ref[which, at * CELLS : (at + 1) * CELLS] = ordered[CELLS:]
 
 
+def append_kernel(odd_ref, near_first_ref, near_second_ref, odds_ref, first_ref, second_ref):
+    odd = odd_ref[0] == 1
+    near = 2 * CELLS
+    for which in range(2):
+        first_ref[which, :near] = near_first_ref[which]
+        second_ref[which, :near] = near_second_ref[which]
+        x = odds_ref[which].astype(F32).reshape(TILE, 2 * TILE, odds_ref.shape[-1])
+        ordered = tile_order(x, odd).astype(BF16)
+        first_ref[which, near:] = ordered[:CELLS]
+        second_ref[which, near:] = ordered[CELLS:]
+
+
 def finish_kernel(odd_ref, mid_ref, first_ref, second_ref, dk_ref, dv_ref):
     odd = odd_ref[0] == 1
     for which, out in ((0, dk_ref), (1, dv_ref)):
@@ -278,7 +290,10 @@
     keys_even, keys_odd = named_swap(keys, keys, "lat")
     (queries,) = call(order_kernel, [odd], [query_field, out_cotangent], [((2, BAND, width), BF16)], 1 << 20, 1 << 20)
     queries_even, queries_odd = named_swap(queries, queries, "lat")
-    first, second = named_swap(*pack(keys, keys_even, keys_odd), "lon")
+    near_first, near_second = pack(keys, keys_even)
+    column = ((2, 3 * CELLS, width), BF16)
+    first, second = call(append_kernel, [odd], [near_first, near_second, keys_odd], [column, column], 1 << 20, 2 << 20)
+    first, second = named_swap(first, second, "lon")
     around = [queries, keys, keys_even, keys_odd, first, second]
     att, stats, low = call(
         attend_kernel, [bias, odd], around,

time: 97.5 us -> 97.3 us (level)
    pallas_call x6 -> x7, Pallas kernels: 14.6 us -> 14.7 us  [call(): pl.pallas_call(kernel, in_specs=[pl.BlockSpec(memory_space=pltpu.SMEM)] *...]
  transfers between devices with their start and end apart: 10 -> 10, of which waited for: 3 -> 3; matrix products, arithmetic and copies ran while one was open for 0% -> 0% of each run, Pallas kernels for 8% -> 9%
where the time goes in v4:
time: 97.3 us; the launch traced here: 96.9 us
  starting transfers between devices  54.2 us (56%)
  waiting for transfers between devices  26.1 us (27%)
  Pallas kernels  14.7 us (15%)
  other arithmetic  1.11 us (1%)
    ppermute x10, starting transfers between devices, swap(): return lax.ppermute(value, axis, pairs)  54.2 us
    ppermute x10, waiting for transfers between devices, swap(): return lax.ppermute(value, axis, pairs)  26.1 us
    pallas_call x7, Pallas kernels, call(): pl.pallas_call(kernel, in_specs=[pl.BlockSpec(memory_space=pltpu.SMEM)] *...  14.7 us
  transfers between devices with their start and end apart: 10, of which 3 were waited for; matrix products, arithmetic and copies ran while one was open for 0% of the time, Pallas kernels for 9%

profile of v4, /device:TPU:55, one launch (start us, length us, event | category | flops | bytes accessed | tf_op | source)
XLA Modules:
  0.0 96.9 jit_solution(46333607336620573)
XLA Ops:
  0.6 0.0 copy-start
  0.6 0.0 copy-start.1
  0.7 1.1 %pad_maximum_fusion.refs_0_.own_ref = bf16[2,128,768]{2,1,0:T(8,128)(2,1)S(1)} fusion(bf16[1,128,768]{2,1,0:T(8,128)(2,1)} %bitcast.4, bf16[1,128,768]{2,1,0:T(8,128)(2,1)} %bitcast.5), kind=kLoop, calls=%fused_computation | loop fusion | flops 196608 | bytes 786432 | tf_op jit(solution)/shard_map/stack | solution.py:289
  1.8 4.0 %collective-permute-start = (bf16[2,128,768]{2,1,0:T(8,128)(2,1)S(1)}, bf16[2,128,768]{2,1,0:T(8,128)(2,1)S(1)}, u32[]{:S(2)}, u32[]{:S(2)}) collective-permute-start(bf16[2,128,768]{2,1,0:T(8,128)(2,1)S(1)} %pad_maximum_fusion.refs_0_.own_ref), channel_id=1, source_target_pairs={{0,32},{32,0},{64,96},{96,64},{128,160},{160,128},{192,224},{224,1... | collective-permute-start | bytes 1179656 | tf_op jit(solution)/shard_map/ppermute | solution.py:269
  5.8 17.5 %collective-permute-start.1 = (bf16[2,128,768]{2,1,0:T(8,128)(2,1)S(1)}, bf16[2,128,768]{2,1,0:T(8,128)(2,1)S(1)}, u32[]{:S(2)}, u32[]{:S(2)}) collective-permute-start(bf16[2,128,768]{2,1,0:T(8,128)(2,1)S(1)} %pad_maximum_fusion.refs_0_.own_ref), channel_id=1, source_target_pairs={{32,64},{64,32},{96,128},{128,96},{160,192},{192,160},{224,256},{2... | collective-permute-start | bytes 1179656 | tf_op jit(solution)/shard_map/ppermute | solution.py:269
  23.3 0.0 collective-permute-done.refs_1_.even_ref
  23.3 0.2 shard_map.76
  23.5 15.6 %collective-permute-done.1.odds_ref = bf16[2,128,768]{2,1,0:T(8,128)(2,1)S(1)} collective-permute-done((bf16[2,128,768]{2,1,0:T(8,128)(2,1)S(1)}, bf16[2,128,768]{2,1,0:T(8,128)(2,1)S(1)}, u32[]{:S(2)}, u32[]{:S(2)}) %collective-permute-start.1) | collective-permute-done | bytes 393248 | tf_op jit(solution)/shard_map/ppermute | solution.py:269
  39.1 1.1 %shard_map.77 = (bf16[2,192,768]{2,1,0:T(8,128)(2,1)}, bf16[2,192,768]{2,1,0:T(8,128)(2,1)}) custom-call(s32[1]{0:T(128)} %bitcast.1.odd_ref, bf16[2,128,768]{2,1,0:T(8,128)(2,1)S(1)} %get-tuple-element.18.near_first_ref, bf16[2,128,768]{2,1,0:T(8,128)(2,1)S(1)} %get-tuple-element.19.near_second_ref, bf16[2,128,768]{2,1,0:T(8,128)(2,1)S(1)} %collective-permute-done.1.odds_ref), custom_call_target="tpu_custom_call" | custom-call | flops 1048576 | bytes 2097152 | tf_op jit(solution)/shard_map/pallas_call | solution.py:252
  40.2 4.4 %collective-permute-start.2 = (bf16[2,192,768]{2,1,0:T(8,128)(2,1)}, bf16[2,192,768]{2,1,0:T(8,128)(2,1)S(1)}, u32[]{:S(2)}, u32[]{:S(2)}) collective-permute-start(bf16[2,192,768]{2,1,0:T(8,128)(2,1)} %get-tuple-element.20), channel_id=1, source_target_pairs={{0,1},{1,0},{2,3},{3,2},{4,5},{5,4},{6,7},{7,6},{8,9},{9,8},{10,11... | collective-permute-start | bytes 1769480 | tf_op jit(solution)/shard_map/ppermute | solution.py:269
  44.7 1.9 %collective-permute-start.3 = (bf16[2,192,768]{2,1,0:T(8,128)(2,1)}, bf16[2,192,768]{2,1,0:T(8,128)(2,1)S(1)}, u32[]{:S(2)}, u32[]{:S(2)}) collective-permute-start(bf16[2,192,768]{2,1,0:T(8,128)(2,1)} %get-tuple-element.21), channel_id=1, source_target_pairs={{1,2},{2,1},{3,4},{4,3},{5,6},{6,5},{7,8},{8,7},{9,10},{10,9},{11,... | collective-permute-start | bytes 1769480 | tf_op jit(solution)/shard_map/ppermute | solution.py:269
  46.6 0.0 copy-done
  46.6 0.0 copy-done.1
  46.6 0.1 shard_map.75.mine_ref
  46.7 1.9 %collective-permute-start.4 = (bf16[2,128,768]{2,1,0:T(8,128)(2,1)S(1)}, bf16[2,128,768]{2,1,0:T(8,128)(2,1)S(1)}, u32[]{:S(2)}, u32[]{:S(2)}) collective-permute-start(bf16[2,128,768]{2,1,0:T(8,128)(2,1)S(1)} %shard_map.75.mine_ref), channel_id=1, source_target_pairs={{0,32},{32,0},{64,96},{96,64},{128,160},{160,128},{192,224},{224,1... | collective-permute-start | bytes 1179656 | tf_op jit(solution)/shard_map/ppermute | solution.py:269
  48.6 9.4 %collective-permute-start.5 = (bf16[2,128,768]{2,1,0:T(8,128)(2,1)S(1)}, bf16[2,128,768]{2,1,0:T(8,128)(2,1)S(1)}, u32[]{:S(2)}, u32[]{:S(2)}) collective-permute-start(bf16[2,128,768]{2,1,0:T(8,128)(2,1)S(1)} %shard_map.75.mine_ref), channel_id=1, source_target_pairs={{32,64},{64,32},{96,128},{128,96},{160,192},{192,160},{224,256},{2... | collective-permute-start | bytes 1179656 | tf_op jit(solution)/shard_map/ppermute | solution.py:269
  58.0 0.0 collective-permute-done.2.first_ref
  58.1 3.3 %collective-permute-done.3.second_ref = bf16[2,192,768]{2,1,0:T(8,128)(2,1)S(1)} collective-permute-done((bf16[2,192,768]{2,1,0:T(8,128)(2,1)}, bf16[2,192,768]{2,1,0:T(8,128)(2,1)S(1)}, u32[]{:S(2)}, u32[]{:S(2)}) %collective-permute-start.3) | collective-permute-done | bytes 589856 | tf_op jit(solution)/shard_map/ppermute | solution.py:269
  61.4 4.6 %shard_map.78 = (bf16[8,16,768]{2,1,0:T(8,128)(2,1)}, f32[6,8,128]{2,1,0:T(8,128)S(1)}, bf16[6,576,256]{2,1,0:T(8,128)(2,1)S(1)}) custom-call(f32[1]{0:T(128)} %bitcast.bias_ref, s32[1]{0:T(128)} %bitcast.1.odd_ref, bf16[2,128,768]{2,1,0:T(8,128)(2,1)S(1)} %shard_map.75.mine_ref, bf16[2,128,768]{2,1,0:T(8,128)(2,1)S(1)} %pad_maximum_fusion.refs_0_.own_ref, ...), custom_call_target="tpu_custom_call" | custom-call | flops 1073741824 | bytes 8388608 | tf_op jit(solution)/shard_map/pallas_call | solution.py:252
  66.0 1.9 %collective-permute-start.6 = (f32[6,8,128]{2,1,0:T(8,128)S(1)}, f32[6,8,128]{2,1,0:T(8,128)S(1)}, u32[]{:S(2)}, u32[]{:S(2)}) collective-permute-start(f32[6,8,128]{2,1,0:T(8,128)S(1)} %get-tuple-element.23.stats_ref), channel_id=1, source_target_pairs={{0,32},{32,0},{64,96},{96,64},{128,160},{160,128},{192,224},{224,1... | collective-permute-start | bytes 73736 | tf_op jit(solution)/shard_map/ppermute | solution.py:269
  67.9 9.4 %collective-permute-start.7 = (f32[6,8,128]{2,1,0:T(8,128)S(1)}, f32[6,8,128]{2,1,0:T(8,128)S(1)}, u32[]{:S(2)}, u32[]{:S(2)}) collective-permute-start(f32[6,8,128]{2,1,0:T(8,128)S(1)} %get-tuple-element.23.stats_ref), channel_id=1, source_target_pairs={{32,64},{64,32},{96,128},{128,96},{160,192},{192,160},{224,256},{2... | collective-permute-start | bytes 73736 | tf_op jit(solution)/shard_map/ppermute | solution.py:269
  77.3 3.4 %shard_map.79 = (bf16[8,16,768]{2,1,0:T(8,128)(2,1)}, f32[2,256,768]{2,1,0:T(8,128)S(1)}) custom-call(s32[1]{0:T(128)} %bitcast.1.odd_ref, bf16[2,128,768]{2,1,0:T(8,128)(2,1)S(1)} %shard_map.75.mine_ref, bf16[2,128,768]{2,1,0:T(8,128)(2,1)S(1)} %pad_maximum_fusion.refs_0_.own_ref, bf16[2,128,768]{2,1,0:T(8,128)(2,1)S(1)} %collective-permute-done.refs_1_.even_ref, ...), custom_call_target="tpu_custom_call" | custom-call | flops 1073741824 | bytes 8388608 | tf_op jit(solution)/shard_map/pallas_call | solution.py:252
  80.7 0.0 collective-permute-done.4.even_ref
  80.7 0.0 collective-permute-done.5.odds_ref
  80.7 0.0 collective-permute-done.6.even_stats
  80.7 0.0 collective-permute-done.7.odds_stats
  80.7 4.4 %shard_map.80 = (f32[2,128,768]{2,1,0:T(8,128)S(1)}, bf16[2,64,768]{2,1,0:T(8,128)(2,1)S(1)}, bf16[2,64,768]{2,1,0:T(8,128)(2,1)S(1)}) custom-call(f32[1]{0:T(128)} %bitcast.bias_ref, bf16[2,128,768]{2,1,0:T(8,128)(2,1)S(1)} %pad_maximum_fusion.refs_0_.own_ref, bf16[2,192,768]{2,1,0:T(8,128)(2,1)S(1)} %collective-permute-done.2.first_ref, ...), custom_call_target="tpu_custom_call" | custom-call | flops 1073741824 | bytes 8388608 | tf_op jit(solution)/shard_map/pallas_call | solution.py:252
  85.1 1.9 %collective-permute-start.8 = (bf16[2,64,768]{2,1,0:T(8,128)(2,1)S(1)}, bf16[2,64,768]{2,1,0:T(8,128)(2,1)S(1)}, u32[]{:S(2)}, u32[]{:S(2)}) collective-permute-start(bf16[2,64,768]{2,1,0:T(8,128)(2,1)S(1)} %get-tuple-element.28), channel_id=1, source_target_pairs={{0,1},{1,0},{2,3},{3,2},{4,5},{5,4},{6,7},{7,6},{8,9},{9,8},{10,11... | collective-permute-start | bytes 589832 | tf_op jit(solution)/shard_map/ppermute | solution.py:269
  87.1 1.9 %collective-permute-start.9 = (bf16[2,64,768]{2,1,0:T(8,128)(2,1)S(1)}, bf16[2,64,768]{2,1,0:T(8,128)(2,1)S(1)}, u32[]{:S(2)}, u32[]{:S(2)}) collective-permute-start(bf16[2,64,768]{2,1,0:T(8,128)(2,1)S(1)} %get-tuple-element.29), channel_id=1, source_target_pairs={{1,2},{2,1},{3,4},{4,3},{5,6},{6,5},{7,8},{8,7},{9,10},{10,9},{11,... | collective-permute-start | bytes 589832 | tf_op jit(solution)/shard_map/ppermute | solution.py:269
  89.0 0.0 collective-permute-done.8.first_ref
  89.0 7.2 %collective-permute-done.9.second_ref = bf16[2,64,768]{2,1,0:T(8,128)(2,1)S(1)} collective-permute-done((bf16[2,64,768]{2,1,0:T(8,128)(2,1)S(1)}, bf16[2,64,768]{2,1,0:T(8,128)(2,1)S(1)}, u32[]{:S(2)}, u32[]{:S(2)}) %collective-permute-start.9) | collective-permute-done | bytes 196640 | tf_op jit(solution)/shard_map/ppermute | solution.py:269
  96.2 0.8 shard_map.81
Async XLA Ops:
  0.6 46.0 %copy-start = (bf16[8,16,768]{2,1,0:T(8,128)(2,1)S(1)}, bf16[8,16,768]{2,1,0:T(8,128)(2,1)}, u32[]{:S(2)}) copy-start(bf16[8,16,768]{2,1,0:T(8,128)(2,1)} %q_ref.1) | copy-start | bytes 589828
  0.6 46.0 %copy-start.1 = (bf16[8,16,768]{2,1,0:T(8,128)(2,1)S(1)}, bf16[8,16,768]{2,1,0:T(8,128)(2,1)}, u32[]{:S(2)}) copy-start(bf16[8,16,768]{2,1,0:T(8,128)(2,1)} %g_ref.1) | copy-start | bytes 589828
  1.8 21.5 %collective-permute-start = (bf16[2,128,768]{2,1,0:T(8,128)(2,1)S(1)}, bf16[2,128,768]{2,1,0:T(8,128)(2,1)S(1)}, u32[]{:S(2)}, u32[]{:S(2)}) collective-permute-start(bf16[2,128,768]{2,1,0:T(8,128)(2,1)S(1)} %pad_maximum_fusion.refs_0_.own_ref), channel_id=1, source_target_pairs={{0,32},{32,0},{64,96},{96,64},{128,160},{160,128},{192,224},{224,1... | collective-permute-start | bytes 1179656 | tf_op jit(solution)/shard_map/ppermute | solution.py:269
  5.8 33.3 %collective-permute-start.1 = (bf16[2,128,768]{2,1,0:T(8,128)(2,1)S(1)}, bf16[2,128,768]{2,1,0:T(8,128)(2,1)S(1)}, u32[]{:S(2)}, u32[]{:S(2)}) collective-permute-start(bf16[2,128,768]{2,1,0:T(8,128)(2,1)S(1)} %pad_maximum_fusion.refs_0_.own_ref), channel_id=1, source_target_pairs={{32,64},{64,32},{96,128},{128,96},{160,192},{192,160},{224,256},{2... | collective-permute-start | bytes 1179656 | tf_op jit(solution)/shard_map/ppermute | solution.py:269
  40.2 17.8 %collective-permute-start.2 = (bf16[2,192,768]{2,1,0:T(8,128)(2,1)}, bf16[2,192,768]{2,1,0:T(8,128)(2,1)S(1)}, u32[]{:S(2)}, u32[]{:S(2)}) collective-permute-start(bf16[2,192,768]{2,1,0:T(8,128)(2,1)} %get-tuple-element.20), channel_id=1, source_target_pairs={{0,1},{1,0},{2,3},{3,2},{4,5},{5,4},{6,7},{7,6},{8,9},{9,8},{10,11... | collective-permute-start | bytes 1769480 | tf_op jit(solution)/shard_map/ppermute | solution.py:269
  44.7 16.7 %collective-permute-start.3 = (bf16[2,192,768]{2,1,0:T(8,128)(2,1)}, bf16[2,192,768]{2,1,0:T(8,128)(2,1)S(1)}, u32[]{:S(2)}, u32[]{:S(2)}) collective-permute-start(bf16[2,192,768]{2,1,0:T(8,128)(2,1)} %get-tuple-element.21), channel_id=1, source_target_pairs={{1,2},{2,1},{3,4},{4,3},{5,6},{6,5},{7,8},{8,7},{9,10},{10,9},{11,... | collective-permute-start | bytes 1769480 | tf_op jit(solution)/shard_map/ppermute | solution.py:269
  46.7 34.0 %collective-permute-start.4 = (bf16[2,128,768]{2,1,0:T(8,128)(2,1)S(1)}, bf16[2,128,768]{2,1,0:T(8,128)(2,1)S(1)}, u32[]{:S(2)}, u32[]{:S(2)}) collective-permute-start(bf16[2,128,768]{2,1,0:T(8,128)(2,1)S(1)} %shard_map.75.mine_ref), channel_id=1, source_target_pairs={{0,32},{32,0},{64,96},{96,64},{128,160},{160,128},{192,224},{224,1... | collective-permute-start | bytes 1179656 | tf_op jit(solution)/shard_map/ppermute | solution.py:269
  48.6 32.0 %collective-permute-start.5 = (bf16[2,128,768]{2,1,0:T(8,128)(2,1)S(1)}, bf16[2,128,768]{2,1,0:T(8,128)(2,1)S(1)}, u32[]{:S(2)}, u32[]{:S(2)}) collective-permute-start(bf16[2,128,768]{2,1,0:T(8,128)(2,1)S(1)} %shard_map.75.mine_ref), channel_id=1, source_target_pairs={{32,64},{64,32},{96,128},{128,96},{160,192},{192,160},{224,256},{2... | collective-permute-start | bytes 1179656 | tf_op jit(solution)/shard_map/ppermute | solution.py:269
  66.0 14.7 %collective-permute-start.6 = (f32[6,8,128]{2,1,0:T(8,128)S(1)}, f32[6,8,128]{2,1,0:T(8,128)S(1)}, u32[]{:S(2)}, u32[]{:S(2)}) collective-permute-start(f32[6,8,128]{2,1,0:T(8,128)S(1)} %get-tuple-element.23.stats_ref), channel_id=1, source_target_pairs={{0,32},{32,0},{64,96},{96,64},{128,160},{160,128},{192,224},{224,1... | collective-permute-start | bytes 73736 | tf_op jit(solution)/shard_map/ppermute | solution.py:269
  67.9 12.8 %collective-permute-start.7 = (f32[6,8,128]{2,1,0:T(8,128)S(1)}, f32[6,8,128]{2,1,0:T(8,128)S(1)}, u32[]{:S(2)}, u32[]{:S(2)}) collective-permute-start(f32[6,8,128]{2,1,0:T(8,128)S(1)} %get-tuple-element.23.stats_ref), channel_id=1, source_target_pairs={{32,64},{64,32},{96,128},{128,96},{160,192},{192,160},{224,256},{2... | collective-permute-start | bytes 73736 | tf_op jit(solution)/shard_map/ppermute | solution.py:269
  85.1 3.9 %collective-permute-start.8 = (bf16[2,64,768]{2,1,0:T(8,128)(2,1)S(1)}, bf16[2,64,768]{2,1,0:T(8,128)(2,1)S(1)}, u32[]{:S(2)}, u32[]{:S(2)}) collective-permute-start(bf16[2,64,768]{2,1,0:T(8,128)(2,1)S(1)} %get-tuple-element.28), channel_id=1, source_target_pairs={{0,1},{1,0},{2,3},{3,2},{4,5},{5,4},{6,7},{7,6},{8,9},{9,8},{10,11... | collective-permute-start | bytes 589832 | tf_op jit(solution)/shard_map/ppermute | solution.py:269
  87.1 9.1 %collective-permute-start.9 = (bf16[2,64,768]{2,1,0:T(8,128)(2,1)S(1)}, bf16[2,64,768]{2,1,0:T(8,128)(2,1)S(1)}, u32[]{:S(2)}, u32[]{:S(2)}) collective-permute-start(bf16[2,64,768]{2,1,0:T(8,128)(2,1)S(1)} %get-tuple-element.29), channel_id=1, source_target_pairs={{1,2},{2,1},{3,4},{4,3},{5,6},{6,5},{7,8},{8,7},{9,10},{10,9},{11,... | collective-permute-start | bytes 589832 | tf_op jit(solution)/shard_map/ppermute | solution.py:269
